TPU v7x, 768 devices: a whole 4x8x12 slice. The times are simulated.
768 devices in a mesh: row: 24 (over z, x_hi), col: 32 (over x_lo, y, core).
Axes of the slice: x: 4 (x_hi: 2, x_lo: 2; x = x_hi * 2 + x_lo), y: 8, z: 12, core: 2. Of those that a mesh axis runs over, the one named last changes fastest.
Arguments:
- object_field: float32 [2, 6144, 8192], P(None, 'row', 'col'), may hold values from -4 to 4
- probe_field: float32 [2, 256, 256], replicated, may hold values from -6 to 6
- measured: float32 [96, 8192, 256], P('row', 'col'), may hold values from 0.1 to 4
- positions: int32 [96, 64], P('row', 'col'), may hold values from 0 to 160
Outputs:
- new_object: float32 [2, 6144, 8192], P(None, 'row', 'col')
- new_probe: float32 [2, 256, 256], replicated
Inputs may be any that keep to these rules, and one draw needn't show every extreme that they name: `positions`: each entry is a pixel offset of a window's top-left corner within its device's tile.
All inputs are finite; a program needn't handle non-finite values.
Results may differ from a plain program's by a relative error of at most 0.0003.
Values sent between devices are 32-bit elements; how exact they have to be, the bound alone decides.
A program may use at most 32 MiB of HBM per device.

v0:
```python
import math

import jax
import jax.numpy as jnp
from jax import lax
from jax.sharding import PartitionSpec as P

HALO = 160


def shifted(value, axis, steps):
    count = lax.axis_size(axis)
    initial, last = (max(0, -steps), min(count, count - steps))
    return lax.ppermute(value, axis, [(source, source + steps) for source in range(initial, last)])


def left_mult(matrix, stack):
    return jnp.einsum("jk,fkl->fjl", matrix, stack, precision=lax.Precision.HIGHEST)


def right_mult(stack, matrix):
    return jnp.einsum("fjk,kl->fjl", stack, matrix, precision=lax.Precision.HIGHEST)


def transform(real_part, imag_part, cosine, sine_part):
    first_re = left_mult(cosine, real_part) - left_mult(sine_part, imag_part)
    first_im = left_mult(cosine, imag_part) + left_mult(sine_part, real_part)
    out_re = right_mult(first_re, cosine) - right_mult(first_im, sine_part)
    out_im = right_mult(first_re, sine_part) + right_mult(first_im, cosine)
    return (out_re, out_im)


def body(object_field, probe_field, measured, positions):
    side = probe_field.shape[1]
    tile = object_field.shape[1]
    margin = HALO
    frames = measured.shape[0]
    right = shifted(object_field[:, :, :margin], "col", -1)
    widened = jnp.concatenate([object_field, right], 2)
    below = shifted(widened[:, :margin, :], "row", -1)
    extended = jnp.concatenate([widened, below], 1)
    zero = jnp.int32(0)
    windows = jnp.stack(
        [
            lax.dynamic_slice(
                extended, (zero, positions[frame, 0], positions[frame, 1]), (2, side, side)
            )
            for frame in range(frames)
        ]
    )
    obj_re = windows[:, 0]
    obj_im = windows[:, 1]
    pro_re = probe_field[0]
    pro_im = probe_field[1]
    wave_re = pro_re * obj_re - pro_im * obj_im
    wave_im = pro_re * obj_im + pro_im * obj_re
    counter = lax.iota(jnp.int32, side)
    product = counter[:, None] * counter[None, :] % side
    angle = 2.0 * math.pi / side * product.astype(jnp.float32)
    scale = 1.0 / math.sqrt(side)
    cosine = jnp.cos(angle) * scale
    sine_fwd = -jnp.sin(angle) * scale
    spec_re, spec_im = transform(wave_re, wave_im, cosine, sine_fwd)
    magnitude = jnp.sqrt(spec_re * spec_re + spec_im * spec_im)
    factor = measured / jnp.maximum(magnitude, 0.5) - 1.0
    change_re, change_im = transform(factor * spec_re, factor * spec_im, cosine, -sine_fwd)
    grad_re = pro_re * change_re + pro_im * change_im
    grad_im = pro_re * change_im - pro_im * change_re
    pieces = jnp.stack([grad_re, grad_im], 1)
    grad_ext = jnp.zeros(extended.shape, jnp.float32)
    for frame in range(frames):
        start = (zero, positions[frame, 0], positions[frame, 1])
        old = lax.dynamic_slice(grad_ext, start, (2, side, side))
        grad_ext = lax.dynamic_update_slice(grad_ext, old + pieces[frame], start)
    probe_re = jnp.sum(obj_re * change_re + obj_im * change_im, 0)
    probe_im = jnp.sum(obj_re * change_im - obj_im * change_re, 0)
    intensity = jnp.sum(obj_re * obj_re + obj_im * obj_im, 0)
    probe_grad = jnp.stack([probe_re, probe_im])
    arrived = shifted(grad_ext[:, tile:, :], "row", 1)
    upper = grad_ext[:, :tile, :]
    upper = upper.at[:, :margin, :].add(arrived)
    sideways = shifted(upper[:, :, tile:], "col", 1)
    grad_tile = upper[:, :, :tile].at[:, :, :margin].add(sideways)
    total_grad, total_inten = lax.psum((probe_grad, intensity), ("row", "col"))
    largest = jnp.max(pro_re * pro_re + pro_im * pro_im)
    new_object = object_field + grad_tile / largest
    new_probe = probe_field + total_grad / (total_inten + 1.0)
    return (new_object, new_probe)


def solution(mesh):
    in_specs = (P(None, "row", "col"), P(), P("row", "col", None), P("row", "col"))
    out_specs = (P(None, "row", "col"), P())
    return jax.shard_map(body, mesh=mesh, in_specs=in_specs, out_specs=out_specs, check_vma=False)
```

profile of v0, /device:TPU:24, one launch (start us, length us, event | category | flops | bytes accessed | tf_op | source)
XLA Modules:
  0.0 626.0 jit_solution(2731846996978270217)
XLA Ops:
  7.2 0.0 all-reduce.3.cloned.1.call-start
  7.2 2.1 collective-permute-start
  9.3 1.1 constant_dynamic-update-slice_fusion.1
  10.4 5.9 collective-permute-done
  16.3 0.1 constant_dynamic-update-slice_fusion
  16.4 1.3 collective-permute-start.1
  17.7 0.7 fusion.139
  33.3 2.2 collective-permute-done.1
  35.5 2.5 fusion.10
  38.0 0.2 pad_maximum_fusion
  38.2 2.8 fusion.46
  41.0 2.8 fusion.50
  43.8 2.8 fusion.3
  46.6 3.1 fusion.48
  49.6 2.7 fusion.33
  52.4 2.8 fusion.2
  55.2 2.7 convolution_subtract_fusion.2
  57.9 3.3 fusion.4
  61.2 2.7 fusion.39
  63.9 2.7 fusion.43
  66.6 2.7 fusion.1
  69.3 2.7 fusion.41
  72.0 2.9 fusion.28
  74.9 2.7 fusion
  77.6 2.7 convolution_subtract_fusion
  80.3 4.1 add_reduce_fusion.1
  84.5 1.4 broadcast_in_dim.2
  85.9 6.7 %dynamic_update_slice.12 = f32[2,416,416]{2,1,0:T(8,128)} dynamic-update-slice(f32[2,416,416]{2,1,0:T(8,128)} %broadcast_in_dim.2, f32[2,256,256]{2,1,0:T(8,128)S(1)} %fusion.19, s32[]{:T(128)} %constant.75.clone.1, s32[]{:T(128)S(6)} %select_n.75, s32[]{:T(128)S(6)} %select_n.76) | dynamic-update-slice | bytes 1048580 | tf_op jit(solution)/shard_map/dynamic_update_slice | solution.py:74
  92.6 1.4 fusion.22
  94.0 6.6 %dynamic_update_slice.13 = f32[2,416,416]{2,1,0:T(8,128)} dynamic-update-slice(f32[2,416,416]{2,1,0:T(8,128)} %dynamic_update_slice.12, f32[2,256,256]{2,1,0:T(8,128)S(1)} %fusion.22, s32[]{:T(128)} %constant.75.clone.1, s32[]{:T(128)S(6)} %select_n.77, s32[]{:T(128)S(6)} %select_n.78) | dynamic-update-slice | bytes 1048580 | tf_op jit(solution)/shard_map/dynamic_update_slice | solution.py:74
  100.6 1.4 fusion.17
  101.9 6.6 %dynamic_update_slice.14 = f32[2,416,416]{2,1,0:T(8,128)} dynamic-update-slice(f32[2,416,416]{2,1,0:T(8,128)} %dynamic_update_slice.13, f32[2,256,256]{2,1,0:T(8,128)S(1)} %fusion.17, s32[]{:T(128)} %constant.75.clone.1, s32[]{:T(128)S(6)} %select_n.79, s32[]{:T(128)S(6)} %select_n.80) | dynamic-update-slice | bytes 1048580 | tf_op jit(solution)/shard_map/dynamic_update_slice | solution.py:74
  108.6 1.4 fusion.24
  109.9 6.7 %dynamic_update_slice.15 = f32[2,416,416]{2,1,0:T(8,128)} dynamic-update-slice(f32[2,416,416]{2,1,0:T(8,128)} %dynamic_update_slice.14, f32[2,256,256]{2,1,0:T(8,128)S(1)} %fusion.24, s32[]{:T(128)} %constant.75.clone.1, s32[]{:T(128)S(6)} %select_n.81, s32[]{:T(128)S(6)} %select_n.82) | dynamic-update-slice | bytes 1048580 | tf_op jit(solution)/shard_map/dynamic_update_slice | solution.py:74
  116.6 2.1 slice.159
  118.7 6.0 collective-permute-start.2
  124.8 0.8 pad_maximum_fusion.2
  125.6 0.7 add_reduce_fusion.2
  126.3 0.1 slice.157
  126.4 12.5 %collective-permute-done.2 = f32[2,160,416]{2,1,0:T(8,128)} collective-permute-done((f32[2,160,416]{2,1,0:T(8,128)}, f32[2,160,416]{2,1,0:T(8,128)}, u32[]{:S(2)}, u32[]{:S(2)}) %collective-permute-start.2) | collective-permute-done | bytes 532512 | tf_op jit(solution)/shard_map/ppermute | solution.py:14
  138.9 1.2 fusion.6
  140.1 2.5 collective-permute-start.3
  142.6 468.3 %all-reduce.3.cloned.1.call-done = (f32[2,256,256]{2,1,0:T(8,128)}, f32[256,256]{1,0:T(8,128)}) async-done(((f32[2,256,256]{2,1,0:T(8,128)}, f32[256,256]{1,0:T(8,128)}), (f32[2,256,256]{2,1,0:T(8,128)}, f32[256,256]{1,0:T(8,128)})) %all-reduce.3.cloned.1.call-update) | async-done | bytes 786448 | tf_op jit(solution)/shard_map/psum | solution.py:84
  610.9 1.0 broadcast_add_fusion
  611.9 1.9 divide_add_fusion.1
  613.9 1.2 slice_add_fusion.1
  615.0 2.2 scatter-add.9
  617.2 1.5 divide_add_fusion.2
  (19 shorter events, 0.2 us)
Async XLA Ops:
  7.2 10.5 %copy-start.4 = (s32[4,2]{0,1:T(2,128)S(1)}, s32[4,2]{0,1:T(2,128)}, u32[]{:S(2)}) copy-start(s32[4,2]{0,1:T(2,128)} %param.11) | copy-start | bytes 100
  7.2 26.1 %copy-start.1 = (f32[2,256,256]{2,1,0:T(8,128)S(1)}, f32[2,256,256]{2,1,0:T(8,128)}, u32[]{:S(2)}) copy-start(f32[2,256,256]{2,1,0:T(8,128)} %param.9) | copy-start | bytes 1572868
  7.2 603.7 %all-reduce.3.cloned.1.call-start = ((), (), s32[]{:S(2)}) async-start(), calls=%async_computation | async-start | bytes 1572864 | tf_op jit(solution)/shard_map/psum | solution.py:84
  7.2 9.1 %collective-permute-start = (f32[2,256,160]{2,1,0:T(8,128)}, f32[2,256,160]{2,1,0:T(8,128)S(1)}, u32[]{:S(2)}, u32[]{:S(2)}) collective-permute-start(f32[2,256,160]{2,1,0:T(8,128)} %bitcast.142), channel_id=1, source_target_pairs={{1,0},{2,1},{3,2},{4,3},{5,4},{6,5},{7,6},{8,7},{9,8},{10,9},{11,1... | collective-permute-start | bytes 983048 | tf_op jit(solution)/shard_map/ppermute | solution.py:14
  16.4 19.1 %collective-permute-start.1 = (f32[2,160,416]{2,1,0:T(8,128)S(1)}, f32[2,160,416]{2,1,0:T(8,128)}, u32[]{:S(2)}, u32[]{:S(2)}) collective-permute-start(f32[2,160,416]{2,1,0:T(8,128)S(1)} %slice.148), channel_id=1, source_target_pairs={{32,0},{64,32},{96,64},{128,96},{160,128},{192,160},{224,192},{256... | collective-permute-start | bytes 1597448 | tf_op jit(solution)/shard_map/ppermute | solution.py:14
  55.2 2.8 copy-start.5
  109.9 14.8 %copy-start.3 = (f32[256,256]{1,0:T(8,128)S(1)}, f32[256,256]{1,0:T(8,128)}, u32[]{:S(2)}) copy-start(f32[256,256]{1,0:T(8,128)} %get-tuple-element.27) | copy-start | bytes 786436
  116.6 9.7 %copy-start = (f32[2,416,416]{2,1,0:T(8,128)S(1)}, f32[2,416,416]{2,1,0:T(8,128)}, u32[]{:S(2)}) copy-start(f32[2,416,416]{2,1,0:T(8,128)} %dynamic_update_slice.15) | copy-start | bytes 4153348
  118.7 20.2 %collective-permute-start.2 = (f32[2,160,416]{2,1,0:T(8,128)}, f32[2,160,416]{2,1,0:T(8,128)}, u32[]{:S(2)}, u32[]{:S(2)}) collective-permute-start(f32[2,160,416]{2,1,0:T(8,128)} %slice.159), channel_id=1, source_target_pairs={{0,32},{32,64},{64,96},{96,128},{128,160},{160,192},{192,224},{224... | collective-permute-start | bytes 1597448 | tf_op jit(solution)/shard_map/ppermute | solution.py:14
  140.1 473.7 %collective-permute-start.3 = (f32[2,256,160]{2,1,0:T(8,128)S(1)}, f32[2,256,160]{2,1,0:T(8,128)}, u32[]{:S(2)}, u32[]{:S(2)}) collective-permute-start(f32[2,256,160]{2,1,0:T(8,128)S(1)} %slice.162), channel_id=1, source_target_pairs={{0,1},{1,2},{2,3},{3,4},{4,5},{5,6},{6,7},{7,8},{8,9},{9,10},{10,1... | collective-permute-start | bytes 983048 | tf_op jit(solution)/shard_map/ppermute | solution.py:14
  613.8 3.4 copy-start.2
Sparse Core Ops, SparseCore 0:
  125.7 485.1 all-reduce.2
where the time goes:
time: 637 us; the launch traced here: 626 us
  waiting for transfers between devices  489 us (77%)
  matrix products  46.1 us (7%)
  local copies, waits for them, and re-layouts  34.4 us (5%)
  between operations  29.6 us (5%)
  other arithmetic  15.1 us (2%)
  starting transfers between devices  11.9 us (2%)
    psum x1, waiting for transfers between devices, body(): total_grad, total_inten = lax.psum((probe_grad, intensity), ('row', 'col'))  468 us
    dynamic_update_slice x4, local copies, waits for them, and re-layouts, body(): grad_ext = lax.dynamic_update_slice(grad_ext, old + pieces[frame], start)  26.6 us
    dot_general x8, matrix products, right_mult(): jnp.einsum('fjk,kl->fjl', stack, matrix, precision=lax.Precision.HIGHEST)  24.3 us
    dot_general x8, matrix products, left_mult(): jnp.einsum('jk,fkl->fjl', matrix, stack, precision=lax.Precision.HIGHEST)  21.8 us
    ppermute x4, waiting for transfers between devices, shifted(): lax.ppermute(value, axis, [(source, source + steps) for source in range(i...  20.6 us
  transfers between devices with their start and end apart: 5, of which 4 were waited for; matrix products, arithmetic and copies ran while one was open for 1% of the time, Pallas kernels for 0%

commit v1 on v0

v1 whole, which is shorter than its diff:
```python
import functools
import math

import jax
import jax.numpy as jnp
import numpy as np
from jax import lax
from jax.experimental import pallas as pl
from jax.experimental.pallas import tpu as pltpu
from jax.sharding import PartitionSpec as P

MESH = pl.DeviceIdType.MESH
DMA = pltpu.SemaphoreType.DMA
F = 256
HALF = 128
HALO = 160
EXT = F + HALO
CHUNKS = 5
TALL = F + 8
WIDE = F + 128
DEEP = EXT + 8
STEP = HALO // CHUNKS
NX, NY, NZ = 4, 8, 12
F32 = jnp.float32
BF16 = jnp.bfloat16
VMEM_SPEC = pl.BlockSpec(memory_space=pltpu.VMEM)
ANY_SPEC = pl.BlockSpec(memory_space=pl.ANY)


class Place:
    def __init__(self):
        self.row = lax.axis_index("row")
        self.col = lax.axis_index("col")
        self.rows = lax.axis_size("row")
        self.cols = lax.axis_size("col")
        self.z = lax.div(self.row, 2)
        self.x = 2 * lax.rem(self.row, 2) + lax.div(self.col, 16)
        self.y = lax.rem(lax.div(self.col, 2), NY)
        self.core = lax.rem(self.col, 2)

    def at(self, x, y, z, core):
        return (2 * z + lax.div(x, 2), 16 * lax.rem(x, 2) + 2 * y + core)

    def partner(self):
        return self.at(self.x, self.y, self.z, 1 - self.core)

    def along_x(self, i):
        return self.at(lax.rem(self.x + i, NX), self.y, self.z, self.core)

    def along_y(self, i):
        return self.at(self.x, lax.rem(self.y + i, NY), self.z, self.core)

    def along_z(self, i):
        return self.at(self.x, self.y, lax.rem(self.z + i, NZ), self.core)

    def up(self):
        return (lax.rem(self.row + self.rows - 1, self.rows), self.col)

    def down(self):
        return (lax.rem(self.row + 1, self.rows), self.col)

    def left(self):
        return (self.row, lax.rem(self.col + self.cols - 1, self.cols))

    def right(self):
        return (self.row, lax.rem(self.col + 1, self.cols))


def meet(devices):
    barrier = pltpu.get_barrier_semaphore()
    for device in devices:
        pl.semaphore_signal(barrier, inc=1, device_id=device, device_id_type=MESH)
    pl.semaphore_wait(barrier, len(devices))


def send(src, dst, send_sem, recv_sem, device):
    copy = pltpu.make_async_remote_copy(
        src_ref=src,
        dst_ref=dst,
        send_sem=send_sem,
        recv_sem=recv_sem,
        device_id=device,
        device_id_type=MESH,
    )
    copy.start()
    return copy


def far_first(count):
    order = []
    for d in range(count // 2, 0, -1):
        order.append(d)
        if count - d != d:
            order.append(count - d)
    return order


def halo_kernel(obj, right, below, corner, row_s, row_r, col_s, col_r, cor_s, cor_r):
    place = Place()
    up, left = place.up(), place.left()
    meet((up, place.down(), left, place.right()))
    rows = []
    for k in range(CHUNKS):
        part = (slice(None), pl.ds(k * STEP, STEP))
        rows.append(send(obj.at[part], below.at[part], row_s.at[k], row_r.at[k], up))
    side = send(obj, right, col_s, col_r, left)
    corners = []
    for k in range(CHUNKS):
        part = (slice(None), pl.ds(k * STEP, STEP))
        rows[k].wait_recv()
        corners.append(
            send(below.at[part], corner.at[part], cor_s.at[k], cor_r.at[k], left)
        )
    side.wait()
    for k in range(CHUNKS):
        rows[k].wait_send()
        corners[k].wait()


def halo_exchange(obj):
    rows = jax.ShapeDtypeStruct((2, HALO, F), F32)
    return pl.pallas_call(
        halo_kernel,
        name="halo",
        out_shape=(jax.ShapeDtypeStruct((2, F, F), F32), rows, rows),
        in_specs=[VMEM_SPEC],
        out_specs=(VMEM_SPEC, VMEM_SPEC, VMEM_SPEC),
        scratch_shapes=[
            DMA((CHUNKS,)),
            DMA((CHUNKS,)),
            DMA,
            DMA,
            DMA((CHUNKS,)),
            DMA((CHUNKS,)),
        ],
        compiler_params=pltpu.CompilerParams(collective_id=0, has_side_effects=True),
    )(obj)


def split(x):
    high = x.astype(BF16)
    return high, (x - high.astype(F32)).astype(BF16)


def dot(a, b):
    return jnp.dot(a, b, preferred_element_type=F32)


def left_mult(high, low, x):
    x_high, x_low = split(x)
    return dot(high, x_high) + (dot(high, x_low) + dot(low, x_high))


def right_mult(x, high, low):
    x_high, x_low = split(x)
    return dot(x_high, high) + (dot(x_low, high) + dot(x_high, low))


def tables():
    k = np.arange(HALF)
    angle = 2.0 * math.pi / HALF * (np.outer(k, k) % HALF)
    cos, sin = np.cos(angle) / 16.0, np.sin(angle) / 16.0
    t1 = np.block([[cos, sin], [-sin, cos]]).astype(np.float32)
    stack = []
    for t in (t1, t1.T):
        high = t.astype(jnp.bfloat16)
        stack += [high, (t - high.astype(np.float32)).astype(jnp.bfloat16)]
    order = np.zeros((F, F), np.float32)
    for v in range(HALF):
        order[2 * v, v] = 1.0
        order[2 * v + 1, HALF + v] = 1.0
    stack.append(order.astype(jnp.bfloat16))
    turn = 2.0 * math.pi / F * k
    down = [np.broadcast_to(f(turn)[:, None], (HALF, HALF)) for f in (np.cos, np.sin)]
    across = [np.broadcast_to(f(turn)[None, :], (8, HALF)) for f in (np.cos, np.sin)]
    twiddle = np.concatenate(down + across, 0).astype(np.float32)
    return np.stack(stack), twiddle


def frame_kernel(
    pos, obj, right, below, corner, probe, measured, mats, twiddle,
    grad, sums, probe_tiles, ext, acc, scale, thin, sems,
):
    frame = pl.program_id(0)
    place = Place()

    @pl.when(frame == 0)
    def _():
        copies = [
            pltpu.make_async_copy(src, ext.at[:, pl.ds(r, n), pl.ds(c, F)], sems.at[i])
            for i, (src, r, n, c) in enumerate(
                ((obj, 0, F, 0), (right, 0, F, F), (below, F, HALO, 0), (corner, F, HALO, F))
            )
        ]
        for copy in copies:
            copy.start()
        grad[...] = jnp.zeros_like(grad)
        acc[...] = jnp.zeros_like(acc)
        p_re, p_im = probe[0], probe[1]
        power = jnp.max(p_re * p_re + p_im * p_im, axis=0, keepdims=True)
        top = jnp.max(power, axis=1, keepdims=True)
        scale[...] = 1.0 / jnp.broadcast_to(top, scale.shape)
        for t in range(32):
            for h in range(2):
                for c in range(2):
                    probe_tiles[2 * t + h, 8 * c : 8 * c + 8] = probe[
                        c, 8 * t : 8 * t + 8, HALF * h : HALF * h + HALF
                    ]
        for copy in copies:
            copy.wait()

        @pl.when(place.col == place.cols - 1)
        def _():
            ext[:, :, F:] = jnp.zeros((2, DEEP, F), F32)

        @pl.when(place.row == place.rows - 1)
        def _():
            ext[:, F:, :] = jnp.zeros((2, DEEP - F, 2 * F), F32)

    dy, dx = pos[frame, 0], pos[frame, 1]
    r_dy, r_dx = lax.rem(dy, 8), lax.rem(dx, HALF)
    rows = pl.ds(pl.multiple_of(dy - r_dy, 8), TALL)
    lanes = pl.ds(pl.multiple_of(dx - r_dx, HALF), WIDE)
    back_dy, back_dx = lax.rem(TALL - r_dy, TALL), lax.rem(WIDE - r_dx, WIDE)

    def window(c):
        return pltpu.roll(pltpu.roll(ext[c, rows, lanes], back_dx, 1)[:, :F], back_dy, 0)[:F]

    o_re, o_im = window(0), window(1)
    p_re, p_im = probe[0], probe[1]
    t1_high, t1_low, t2_high, t2_low, order = (mats[i] for i in range(5))
    down_c = jnp.concatenate([twiddle[:HALF]] * 2, 1)
    down_s = jnp.concatenate([twiddle[HALF:F]] * 2, 1)
    over_c, over_s = twiddle[F : F + 1], twiddle[F + 8 : F + 9]

    for h in range(2):
        thin[h] = measured[0, :, HALF * h : HALF * h + HALF]
    even = [thin[h, pl.ds(0, HALF, 2), :] for h in range(2)]
    odd = [thin[h, pl.ds(1, HALF, 2), :] for h in range(2)]
    sorted_rows = jnp.concatenate([jnp.concatenate(even, 1), jnp.concatenate(odd, 1)], 0)
    m_high, m_low = split(sorted_rows)
    ampl = dot(m_high, order) + dot(m_low, order)

    w_re = p_re * o_re - p_im * o_im
    w_im = p_re * o_im + p_im * o_re
    d_re, d_im = w_re[:HALF] - w_re[HALF:], w_im[:HALF] - w_im[HALF:]
    a = jnp.concatenate([w_re[:HALF] + w_re[HALF:], w_im[:HALF] + w_im[HALF:]], 0)
    b = jnp.concatenate([d_re * down_c + d_im * down_s, d_im * down_c - d_re * down_s], 0)
    y_even, y_odd = left_mult(t1_high, t1_low, a), left_mult(t1_high, t1_low, b)
    x_re = jnp.concatenate([y_even[:HALF], y_odd[:HALF]], 0)
    x_im = jnp.concatenate([y_even[HALF:], y_odd[HALF:]], 0)
    d_re, d_im = x_re[:, :HALF] - x_re[:, HALF:], x_im[:, :HALF] - x_im[:, HALF:]
    a = jnp.concatenate([x_re[:, :HALF] + x_re[:, HALF:], x_im[:, :HALF] + x_im[:, HALF:]], 1)
    b = jnp.concatenate([d_re * over_c + d_im * over_s, d_im * over_c - d_re * over_s], 1)

    def fit(x, target):
        re, im = x[:, :HALF], x[:, HALF:]
        factor = target * jnp.minimum(lax.rsqrt(re * re + im * im), 2.0) - 1.0
        return jnp.concatenate([re * factor, im * factor], 1)

    s_even = fit(right_mult(a, t2_high, t2_low), ampl[:, :HALF])
    s_odd = fit(right_mult(b, t2_high, t2_low), ampl[:, HALF:])
    e, o = right_mult(s_even, t1_high, t1_low), right_mult(s_odd, t1_high, t1_low)
    e_re, e_im, o_re2, o_im2 = e[:, :HALF], e[:, HALF:], o[:, :HALF], o[:, HALF:]
    q_re, q_im = o_re2 * over_c - o_im2 * over_s, o_im2 * over_c + o_re2 * over_s
    x_re = jnp.concatenate([e_re + q_re, e_re - q_re], 1)
    x_im = jnp.concatenate([e_im + q_im, e_im - q_im], 1)
    e = left_mult(t2_high, t2_low, jnp.concatenate([x_re[:HALF], x_im[:HALF]], 0))
    o = left_mult(t2_high, t2_low, jnp.concatenate([x_re[HALF:], x_im[HALF:]], 0))
    e_re, e_im, o_re2, o_im2 = e[:HALF], e[HALF:], o[:HALF], o[HALF:]
    q_re, q_im = o_re2 * down_c - o_im2 * down_s, o_im2 * down_c + o_re2 * down_s
    c_re = jnp.concatenate([e_re + q_re, e_re - q_re], 0)
    c_im = jnp.concatenate([e_im + q_im, e_im - q_im], 0)

    acc[0] += o_re * c_re + o_im * c_im
    acc[1] += o_re * c_im - o_im * c_re
    acc[2] += o_re * o_re + o_im * o_im
    inverse = scale[0:1, 0:1]
    blank_rows, blank_lanes = jnp.zeros((TALL - F, F), F32), jnp.zeros((TALL, WIDE - F), F32)
    for c, g in ((0, p_re * c_re + p_im * c_im), (1, p_re * c_im - p_im * c_re)):
        moved = pltpu.roll(jnp.concatenate([g * inverse, blank_rows], 0), r_dy, 0)
        moved = pltpu.roll(jnp.concatenate([moved, blank_lanes], 1), r_dx, 1)
        grad[c, rows, lanes] += moved

    @pl.when(frame == pl.num_programs(0) - 1)
    def _():
        for t in range(32):
            for h in range(2):
                for c in range(3):
                    sums[2 * t + h, 8 * c : 8 * c + 8] = acc[
                        c, 8 * t : 8 * t + 8, HALF * h : HALF * h + HALF
                    ]


def frame_step(positions, obj, right, below, corner, probe, measured):
    mats, twiddle = tables()

    def whole(shape):
        return pl.BlockSpec(shape, lambda f: (0,) * len(shape))

    return pl.pallas_call(
        frame_kernel,
        name="frames",
        grid=(measured.shape[0],),
        out_shape=(
            jax.ShapeDtypeStruct((2, DEEP, 2 * F), F32),
            jax.ShapeDtypeStruct((64, 24, HALF), F32),
            jax.ShapeDtypeStruct((64, 16, HALF), F32),
        ),
        in_specs=[
            pl.BlockSpec(memory_space=pltpu.SMEM),
            ANY_SPEC,
            ANY_SPEC,
            ANY_SPEC,
            ANY_SPEC,
            whole((2, F, F)),
            pl.BlockSpec((1, F, F), lambda f: (f, 0, 0)),
            whole((5, F, F)),
            whole((F + 16, HALF)),
        ],
        out_specs=(whole((2, DEEP, 2 * F)), whole((64, 24, HALF)), whole((64, 16, HALF))),
        scratch_shapes=[
            pltpu.VMEM((2, DEEP, 2 * F), F32),
            pltpu.VMEM((3, F, F), F32),
            pltpu.VMEM((8, HALF), F32),
            pltpu.VMEM((2, F, HALF), F32),
            DMA((4,)),
        ],
    )(positions, obj, right, below, corner, probe, measured, jnp.asarray(mats), jnp.asarray(twiddle))


def reduce_kernel(
    grad, sums, probe_tiles, obj, new_obj, new_probe,
    main, side, below, bottom, core_in, half, y_in, y_sum, x_in, x_sum, z_in, tiles,
    local_s, core_s, core_r, y_s, y_r, x_s, x_r, z_s, z_r, xg_s, xg_r, yg_s, yg_r, cg_s, cg_r,
    side_s, side_r, bot_s, bot_r,
):
    place = Place()
    core, x, y, z = place.core, place.x, place.y, place.z
    partner, right, down = place.partner(), place.right(), place.down()
    peers = [partner, right, place.left(), down, place.up()]
    peers += [place.along_x(i) for i in range(1, NX)]
    peers += [place.along_y(i) for i in range(1, NY)]
    peers += [place.along_z(i) for i in range(1, NZ)]
    meet(peers)

    fetch = pltpu.make_async_copy(grad.at[:, pl.ds(0, EXT), pl.ds(0, F)], main, local_s)
    fetch.start()
    first = send(sums.at[pl.ds(32 * (1 - core), 32)], core_in, core_s, core_r, partner)
    first.wait()
    half[...] = sums[pl.ds(32 * core, 32)] + core_in[...]

    y_out = []
    for i in far_first(NY):
        there = lax.rem(y + i, NY)
        y_out.append(
            send(half.at[pl.ds(4 * there, 4)], y_in.at[i - 1], y_s.at[i], y_r.at[i], place.along_y(i))
        )
    for copy in y_out:
        copy.wait()
    total = half[pl.ds(4 * y, 4)]
    for i in range(NY - 1):
        total = total + y_in[i]
    y_sum[...] = total

    x_out = []
    for i in far_first(NX):
        there = lax.rem(x + i, NX)
        x_out.append(send(y_sum.at[there], x_in.at[i - 1], x_s.at[i], x_r.at[i], place.along_x(i)))
    side_out = []
    for k in range(CHUNKS + 1):
        part = (slice(None), pl.ds(F + k * STEP, STEP) if k < CHUNKS else pl.ds(0, F))
        src = grad.at[part + (pl.ds(F, F),)]
        side_out.append(send(src, side.at[part], side_s.at[k], side_r.at[k], right))
    for copy in x_out:
        copy.wait()
    x_sum[...] = ((y_sum[x] + x_in[0]) + x_in[1]) + x_in[2]

    z_out = []
    for i in far_first(NZ):
        z_out.append(send(x_sum, z_in.at[z], z_s.at[i], z_r.at[i], place.along_z(i)))
    z_in[z] = x_sum[...]

    fetch.wait()
    first_col = place.col == 0
    bottom_out = []
    for k in range(CHUNKS):
        side_out[k].wait()
        rows = pl.ds(F + k * STEP, STEP)
        extra = jnp.where(first_col, 0.0, side[:, rows, :])
        bottom[:, pl.ds(k * STEP, STEP), :] = main[:, rows, :] + extra
        part = (slice(None), pl.ds(k * STEP, STEP))
        bottom_out.append(send(bottom.at[part], below.at[part], bot_s.at[k], bot_r.at[k], down))

    for copy in z_out:
        copy.wait()
    total = z_in[0]
    for i in range(1, NZ):
        total = total + z_in[i]
    mine = 32 * core + 4 * y + x
    bar = total[16:24] + 1.0
    step = jnp.concatenate([total[0:8] / bar, total[8:16] / bar], 0)
    tiles[mine] = probe_tiles[mine] + step

    xg_out = []
    for i in far_first(NX):
        xg_out.append(send(tiles.at[mine], tiles.at[mine], xg_s.at[i], xg_r.at[i], place.along_x(i)))
    for copy in xg_out:
        copy.wait()
    block = pl.ds(32 * core + 4 * y, 4)
    yg_out = {}
    for i in far_first(NY):
        yg_out[i] = send(tiles.at[block], tiles.at[block], yg_s.at[i], yg_r.at[i], place.along_y(i))
    cg_out = [send(tiles.at[block], tiles.at[block], cg_s.at[0], cg_r.at[0], partner)]
    order = sorted(yg_out, key=lambda i: min(i, NY - i))
    for i in order:
        yg_out[i].wait_recv()
        came = lax.rem(y + NY - i, NY)
        part = pl.ds(32 * core + 4 * came, 4)
        cg_out.append(send(tiles.at[part], tiles.at[part], cg_s.at[i], cg_r.at[i], partner))

    side_out[CHUNKS].wait()
    new_obj[...] = obj[...] + (main[:, pl.ds(0, F), :] + jnp.where(first_col, 0.0, side[:, pl.ds(0, F), :]))
    for copy in bottom_out:
        copy.wait()
    first_row = place.row == 0
    new_obj[:, pl.ds(0, HALO), :] += jnp.where(first_row, 0.0, below[...])

    for i in order:
        yg_out[i].wait_send()
    for copy in cg_out:
        copy.wait()
    for t in range(32):
        for h in range(2):
            for c in range(2):
                new_probe[c, 8 * t : 8 * t + 8, HALF * h : HALF * h + HALF] = tiles[
                    2 * t + h, 8 * c : 8 * c + 8
                ]


def reduce_step(grad, sums, probe_tiles, obj):
    out = jax.ShapeDtypeStruct((2, F, F), F32)

    def vmem(*shape):
        return pltpu.VMEM(shape, F32)

    return pl.pallas_call(
        reduce_kernel,
        name="reduce",
        out_shape=(out, out),
        in_specs=[ANY_SPEC, VMEM_SPEC, VMEM_SPEC, VMEM_SPEC],
        out_specs=(VMEM_SPEC, VMEM_SPEC),
        scratch_shapes=[
            vmem(2, EXT, F),
            vmem(2, EXT, F),
            vmem(2, HALO, F),
            vmem(2, HALO, F),
            vmem(32, 24, HALF),
            vmem(32, 24, HALF),
            vmem(NY - 1, 4, 24, HALF),
            vmem(4, 24, HALF),
            vmem(NX - 1, 24, HALF),
            vmem(24, HALF),
            vmem(NZ, 24, HALF),
            vmem(64, 16, HALF),
            DMA,
            DMA,
            DMA,
            *[DMA((n,)) for n in (NY, NY, NX, NX, NZ, NZ, NX, NX, NY, NY, NY, NY)],
            DMA((CHUNKS + 1,)),
            DMA((CHUNKS + 1,)),
            DMA((CHUNKS,)),
            DMA((CHUNKS,)),
        ],
        compiler_params=pltpu.CompilerParams(collective_id=1, has_side_effects=True),
    )(grad, sums, probe_tiles, obj)


def body(object_field, probe_field, measured, positions):
    right, below, corner = halo_exchange(object_field)
    pos = positions.reshape(measured.shape[0], 2)
    grad, sums, probe_tiles = frame_step(
        pos, object_field, right, below, corner, probe_field, measured
    )
    return reduce_step(grad, sums, probe_tiles, object_field)


def solution(mesh):
    in_specs = (P(None, "row", "col"), P(), P("row", "col", None), P("row", "col"))
    out_specs = (P(None, "row", "col"), P())
    return jax.shard_map(body, mesh=mesh, in_specs=in_specs, out_specs=out_specs, check_vma=False)
```

time: 637 us -> 110 us (0.17)
  the two profiles are of different devices: /device:TPU:24 before, /device:TPU:9 now
where the time goes in v1:
time: 110 us
  Pallas kernels  104 us (95%)
  local copies, waits for them, and re-layouts  5.07 us (5%)
    pallas_call x1, Pallas kernels, reduce_step(): pl.pallas_call(reduce_kernel, name='reduce', out_shape=(out, out), in_spe...  59.3 us
    pallas_call x1, Pallas kernels, halo_exchange(): pl.pallas_call(halo_kernel, name='halo', out_shape=(jax.ShapeDtypeStruct(...  30.3 us
    pallas_call x1, Pallas kernels, frame_step(): pl.pallas_call(frame_kernel, name='frames', grid=(measured.shape[0],), ou...  14.2 us
    unnamed x3, local copies, waits for them, and re-layouts  5.07 us

profile of v1, /device:TPU:9, one launch (start us, length us, event | category | flops | bytes accessed | tf_op | source)
XLA Modules:
  0.0 109.5 jit_solution(13015925487705410544)
XLA Ops:
  0.6 1.3 %copy.8.pos = s32[4,2]{1,0:T(4,128)} copy(s32[4,2]{0,1:T(2,128)} %param.9) | data formatting | bytes 64 | tf_op args[3]
  2.0 30.3 %halo.1 = (f32[2,256,256]{2,1,0:T(8,128)}, f32[2,160,256]{2,1,0:T(8,128)}, f32[2,160,256]{2,1,0:T(8,128)}) custom-call(f32[2,256,256]{2,1,0:T(8,128)} %obj.5), custom_call_target="tpu_custom_call" | custom-call | tf_op jit(solution)/shard_map/halo/pallas_call | solution.py:122
  32.3 14.2 %frames.1 = (f32[2,424,512]{2,1,0:T(8,128)}, f32[64,24,128]{2,1,0:T(8,128)}, f32[64,16,128]{2,1,0:T(8,128)}) custom-call(s32[4,2]{1,0:T(4,128)} %copy.8.pos, f32[2,256,256]{2,1,0:T(8,128)} %obj.5, f32[2,256,256]{2,1,0:T(8,128)} %get-tuple-element.8.right, f32[2,160,256]{2,1,0:T(8,128)} %get-tuple-element.9.below, f32[2,160,256]{2,1,0:T(8,128)} %get-tuple-element.10.corner, ...), custom_call_target="tpu_custom_call" | custom-call | tf_op jit(solution)/shard_map/frames/pallas_call | solution.py:301
  46.5 59.3 %reduce.1 = (f32[2,256,256]{2,1,0:T(8,128)}, f32[2,256,256]{2,1,0:T(8,128)}) custom-call(f32[2,424,512]{2,1,0:T(8,128)} %get-tuple-element.11.grad, f32[64,24,128]{2,1,0:T(8,128)} %get-tuple-element.12.sums, f32[64,16,128]{2,1,0:T(8,128)} %get-tuple-element.13.probe_tiles, f32[2,256,256]{2,1,0:T(8,128)} %obj.5), custom_call_target="tpu_custom_call" | custom-call | tf_op jit(solution)/shard_map/reduce/pallas_call | solution.py:447
  105.8 1.9 %copy.11 = f32[2,256,256]{2,1,0:T(8,128)} copy(f32[2,256,256]{2,1,0:T(8,128)} %get-tuple-element.16) | data formatting | bytes 1048576
  107.6 1.9 %copy.12 = f32[2,256,256]{2,1,0:T(8,128)} copy(f32[2,256,256]{2,1,0:T(8,128)} %get-tuple-element.17) | data formatting | bytes 1048576

commit v2 on v1

v2 whole, which is shorter than its diff:
```python
import functools
import math

import jax
import jax.numpy as jnp
import numpy as np
from jax import lax
from jax.experimental import pallas as pl
from jax.experimental.pallas import tpu as pltpu
from jax.sharding import PartitionSpec as P

MESH = pl.DeviceIdType.MESH
DMA = pltpu.SemaphoreType.DMA
F = 256
HALF = 128
HALO = 160
EXT = F + HALO
CHUNKS = 5
TALL = F + 8
WIDE = F + 128
DEEP = EXT + 8
STEP = HALO // CHUNKS
NX, NY, NZ = 4, 8, 12
COMPONENTS = (2, 0, 1)
F32 = jnp.float32
BF16 = jnp.bfloat16
VMEM_SPEC = pl.BlockSpec(memory_space=pltpu.VMEM)
ANY_SPEC = pl.BlockSpec(memory_space=pl.ANY)


class Place:
    def __init__(self):
        self.row = lax.axis_index("row")
        self.col = lax.axis_index("col")
        self.rows = lax.axis_size("row")
        self.cols = lax.axis_size("col")
        self.z = lax.div(self.row, 2)
        self.x = 2 * lax.rem(self.row, 2) + lax.div(self.col, 16)
        self.y = lax.rem(lax.div(self.col, 2), NY)
        self.core = lax.rem(self.col, 2)

    def at(self, x, y, z, core):
        return (2 * z + lax.div(x, 2), 16 * lax.rem(x, 2) + 2 * y + core)

    def partner(self):
        return self.at(self.x, self.y, self.z, 1 - self.core)

    def along_x(self, i):
        return self.at(lax.rem(self.x + i, NX), self.y, self.z, self.core)

    def along_y(self, i):
        return self.at(self.x, lax.rem(self.y + i, NY), self.z, self.core)

    def along_z(self, i):
        return self.at(self.x, self.y, lax.rem(self.z + i, NZ), self.core)

    def up(self):
        return (lax.rem(self.row + self.rows - 1, self.rows), self.col)

    def down(self):
        return (lax.rem(self.row + 1, self.rows), self.col)

    def left(self):
        return (self.row, lax.rem(self.col + self.cols - 1, self.cols))

    def right(self):
        return (self.row, lax.rem(self.col + 1, self.cols))


def meet(devices):
    barrier = pltpu.get_barrier_semaphore()
    for device in devices:
        pl.semaphore_signal(barrier, inc=1, device_id=device, device_id_type=MESH)
    pl.semaphore_wait(barrier, len(devices))


def send(src, dst, send_sem, recv_sem, device):
    copy = pltpu.make_async_remote_copy(
        src_ref=src,
        dst_ref=dst,
        send_sem=send_sem,
        recv_sem=recv_sem,
        device_id=device,
        device_id_type=MESH,
    )
    copy.start()
    return copy


def far_first(count):
    order = []
    for d in range(count // 2, 0, -1):
        order.append(d)
        if count - d != d:
            order.append(count - d)
    return order


def halo_kernel(
    obj, probe, measured, mats, twiddle, ext, ampl, probe_out, mats_out, twiddle_out,
    raw, row_s, row_r, col_s, col_r, cor_s, cor_r, own_s,
):
    place = Place()
    up, left = place.up(), place.left()
    loads = [
        pltpu.make_async_copy(src, dst, own_s.at[i])
        for i, (src, dst) in enumerate(
            (
                (measured, raw),
                (mats, mats_out),
                (obj, ext.at[:, pl.ds(0, F), pl.ds(0, F)]),
                (probe, probe_out),
                (twiddle, twiddle_out),
            )
        )
    ]
    for load in loads:
        load.start()
    meet((up, place.down(), left, place.right()))
    rows = []
    for k in range(CHUNKS):
        here, there = pl.ds(k * STEP, STEP), pl.ds(F + k * STEP, STEP)
        dst = ext.at[:, there, pl.ds(0, F)]
        rows.append(send(obj.at[:, here], dst, row_s.at[k], row_r.at[k], up))
    side = send(obj, ext.at[:, pl.ds(0, F), pl.ds(F, F)], col_s, col_r, left)

    loads[0].wait()
    loads[1].wait()
    across, down = mats_out[4], mats_out[5]

    def reorder(f, carry):
        parts = [dot(down, part).astype(BF16) for part in split(raw[f])]
        ampl[f] = dot(parts[0], across) + dot(parts[1], across)
        return carry

    lax.fori_loop(0, raw.shape[0], reorder, 0)

    corners = []
    for k in range(CHUNKS):
        there = pl.ds(F + k * STEP, STEP)
        src, dst = ext.at[:, there, pl.ds(0, F)], ext.at[:, there, pl.ds(F, F)]
        rows[k].wait_recv()
        corners.append(send(src, dst, cor_s.at[k], cor_r.at[k], left))
    for load in loads[2:]:
        load.wait()
    side.wait()
    for k in range(CHUNKS):
        rows[k].wait_send()
        corners[k].wait()

    @pl.when(place.col == place.cols - 1)
    def _():
        ext[:, :, F:] = jnp.zeros((2, DEEP, F), F32)

    @pl.when(place.row == place.rows - 1)
    def _():
        ext[:, F:, :] = jnp.zeros((2, DEEP - F, 2 * F), F32)


def in_hbm(array):
    return pltpu.with_memory_space_constraint(array, pltpu.HBM)


def halo_exchange(obj, probe, measured):
    mats, twiddle = tables()
    like = jax.ShapeDtypeStruct
    frames = measured.shape[0]
    return pl.pallas_call(
        halo_kernel,
        name="halo",
        out_shape=(
            like((2, DEEP, 2 * F), F32),
            like((frames, F, F), F32),
            like((2, F, F), F32),
            like(mats.shape, BF16),
            like(twiddle.shape, F32),
        ),
        in_specs=[pl.BlockSpec(memory_space=pltpu.HBM)] * 5,
        out_specs=(VMEM_SPEC,) * 5,
        scratch_shapes=[
            pltpu.VMEM((frames, F, F), F32),
            DMA((CHUNKS,)),
            DMA((CHUNKS,)),
            DMA,
            DMA,
            DMA((CHUNKS,)),
            DMA((CHUNKS,)),
            DMA((5,)),
        ],
        compiler_params=pltpu.CompilerParams(
            collective_id=0, has_side_effects=True, vmem_limit_bytes=12 << 20
        ),
    )(*(in_hbm(a) for a in (obj, probe, measured, jnp.asarray(mats), jnp.asarray(twiddle))))


def split(x):
    high = x.astype(BF16)
    return high, (x - high.astype(F32)).astype(BF16)


def dot(a, b):
    return jnp.dot(a, b, preferred_element_type=F32)


def left_mult(high, low, x):
    x_high, x_low = split(x)
    return dot(high, x_high) + (dot(high, x_low) + dot(low, x_high))


def right_mult(x, high, low):
    x_high, x_low = split(x)
    return dot(x_high, high) + (dot(x_low, high) + dot(x_high, low))


def tables():
    k = np.arange(HALF)
    angle = 2.0 * math.pi / HALF * (np.outer(k, k) % HALF)
    cos, sin = np.cos(angle) / 16.0, np.sin(angle) / 16.0
    t1 = np.block([[cos, sin], [-sin, cos]]).astype(np.float32)
    stack = []
    for t in (t1, t1.T):
        high = t.astype(jnp.bfloat16)
        stack += [high, (t - high.astype(np.float32)).astype(jnp.bfloat16)]
    order = np.zeros((F, F), np.float32)
    for v in range(HALF):
        order[2 * v, v] = 1.0
        order[2 * v + 1, HALF + v] = 1.0
    stack += [order.astype(jnp.bfloat16), order.T.astype(jnp.bfloat16)]
    turn = 2.0 * math.pi / F * k
    down = [np.broadcast_to(f(turn)[:, None], (HALF, HALF)) for f in (np.cos, np.sin)]
    across = [np.broadcast_to(f(turn)[None, :], (8, HALF)) for f in (np.cos, np.sin)]
    twiddle = np.concatenate(down + across, 0).astype(np.float32)
    return np.stack(stack), twiddle


def frame_kernel(
    pos, ext, ampl, probe, mats, twiddle, grad, sums, probe_tiles, acc, scale
):
    frame = pl.program_id(0)

    @pl.when(frame == 0)
    def _():
        grad[...] = jnp.zeros_like(grad)
        acc[...] = jnp.zeros_like(acc)
        p_re, p_im = probe[0], probe[1]
        power = jnp.max(p_re * p_re + p_im * p_im, axis=0, keepdims=True)
        top = jnp.max(power, axis=1, keepdims=True)
        scale[...] = 1.0 / jnp.broadcast_to(top, scale.shape)
        for t in range(32):
            for h in range(2):
                for c in range(2):
                    probe_tiles[2 * t + h, 8 * c : 8 * c + 8] = probe[
                        c, 8 * t : 8 * t + 8, HALF * h : HALF * h + HALF
                    ]

    dy, dx = pos[0, frame], pos[1, frame]
    r_dy, r_dx = lax.rem(dy, 8), lax.rem(dx, HALF)
    rows = pl.ds(pl.multiple_of(dy - r_dy, 8), TALL)
    lanes = pl.ds(pl.multiple_of(dx - r_dx, HALF), WIDE)
    back_dy, back_dx = lax.rem(TALL - r_dy, TALL), lax.rem(WIDE - r_dx, WIDE)

    def window(c):
        return pltpu.roll(pltpu.roll(ext[c, rows, lanes], back_dx, 1)[:, :F], back_dy, 0)[:F]

    o_re, o_im = window(0), window(1)
    p_re, p_im = probe[0], probe[1]
    t1_high, t1_low, t2_high, t2_low = (mats[i] for i in range(4))
    down_c = jnp.concatenate([twiddle[:HALF]] * 2, 1)
    down_s = jnp.concatenate([twiddle[HALF:F]] * 2, 1)
    over_c, over_s = twiddle[F : F + 1], twiddle[F + 8 : F + 9]

    w_re = p_re * o_re - p_im * o_im
    w_im = p_re * o_im + p_im * o_re
    d_re, d_im = w_re[:HALF] - w_re[HALF:], w_im[:HALF] - w_im[HALF:]
    a = jnp.concatenate([w_re[:HALF] + w_re[HALF:], w_im[:HALF] + w_im[HALF:]], 0)
    b = jnp.concatenate([d_re * down_c + d_im * down_s, d_im * down_c - d_re * down_s], 0)
    y_even, y_odd = left_mult(t1_high, t1_low, a), left_mult(t1_high, t1_low, b)
    x_re = jnp.concatenate([y_even[:HALF], y_odd[:HALF]], 0)
    x_im = jnp.concatenate([y_even[HALF:], y_odd[HALF:]], 0)
    d_re, d_im = x_re[:, :HALF] - x_re[:, HALF:], x_im[:, :HALF] - x_im[:, HALF:]
    a = jnp.concatenate([x_re[:, :HALF] + x_re[:, HALF:], x_im[:, :HALF] + x_im[:, HALF:]], 1)
    b = jnp.concatenate([d_re * over_c + d_im * over_s, d_im * over_c - d_re * over_s], 1)

    def fit(x, target):
        re, im = x[:, :HALF], x[:, HALF:]
        factor = target * jnp.minimum(lax.rsqrt(re * re + im * im), 2.0) - 1.0
        return jnp.concatenate([re * factor, im * factor], 1)

    s_even = fit(right_mult(a, t2_high, t2_low), ampl[0, :, :HALF])
    s_odd = fit(right_mult(b, t2_high, t2_low), ampl[0, :, HALF:])
    e, o = right_mult(s_even, t1_high, t1_low), right_mult(s_odd, t1_high, t1_low)
    e_re, e_im, o_re2, o_im2 = e[:, :HALF], e[:, HALF:], o[:, :HALF], o[:, HALF:]
    q_re, q_im = o_re2 * over_c - o_im2 * over_s, o_im2 * over_c + o_re2 * over_s
    x_re = jnp.concatenate([e_re + q_re, e_re - q_re], 1)
    x_im = jnp.concatenate([e_im + q_im, e_im - q_im], 1)
    e = left_mult(t2_high, t2_low, jnp.concatenate([x_re[:HALF], x_im[:HALF]], 0))
    o = left_mult(t2_high, t2_low, jnp.concatenate([x_re[HALF:], x_im[HALF:]], 0))
    e_re, e_im, o_re2, o_im2 = e[:HALF], e[HALF:], o[:HALF], o[HALF:]
    q_re, q_im = o_re2 * down_c - o_im2 * down_s, o_im2 * down_c + o_re2 * down_s
    c_re = jnp.concatenate([e_re + q_re, e_re - q_re], 0)
    c_im = jnp.concatenate([e_im + q_im, e_im - q_im], 0)

    acc[0] += o_re * c_re + o_im * c_im
    acc[1] += o_re * c_im - o_im * c_re
    acc[2] += o_re * o_re + o_im * o_im
    inverse = scale[0:1, 0:1]
    blank_rows, blank_lanes = jnp.zeros((TALL - F, F), F32), jnp.zeros((TALL, WIDE - F), F32)
    for c, g in ((0, p_re * c_re + p_im * c_im), (1, p_re * c_im - p_im * c_re)):
        moved = pltpu.roll(jnp.concatenate([g * inverse, blank_rows], 0), r_dy, 0)
        moved = pltpu.roll(jnp.concatenate([moved, blank_lanes], 1), r_dx, 1)
        grad[c, rows, lanes] += moved

    @pl.when(frame == pl.num_programs(0) - 1)
    def _():
        for t in range(32):
            for h in range(2):
                for c in range(3):
                    sums[c, 2 * t + h] = acc[
                        c, 8 * t : 8 * t + 8, HALF * h : HALF * h + HALF
                    ]


def frame_step(positions, ext, ampl, probe, mats, twiddle):
    def whole(shape):
        return pl.BlockSpec(shape, lambda f: (0,) * len(shape))

    return pl.pallas_call(
        frame_kernel,
        name="frames",
        grid=(ampl.shape[0],),
        out_shape=(
            jax.ShapeDtypeStruct((2, DEEP, 2 * F), F32),
            jax.ShapeDtypeStruct((3, 64, 8, HALF), F32),
            jax.ShapeDtypeStruct((64, 16, HALF), F32),
        ),
        in_specs=[
            pl.BlockSpec(memory_space=pltpu.SMEM),
            whole((2, DEEP, 2 * F)),
            pl.BlockSpec((1, F, F), lambda f: (f, 0, 0)),
            whole((2, F, F)),
            whole(mats.shape),
            whole(twiddle.shape),
        ],
        out_specs=(whole((2, DEEP, 2 * F)), whole((3, 64, 8, HALF)), whole((64, 16, HALF))),
        scratch_shapes=[pltpu.VMEM((3, F, F), F32), pltpu.VMEM((8, HALF), F32)],
        compiler_params=pltpu.CompilerParams(vmem_limit_bytes=28 << 20),
    )(positions, ext, ampl, probe, mats, twiddle)


def reduce_kernel(
    grad, sums, probe_tiles, grad_sum, tiles,
    main, side, below, bottom, core_in, half, x_in, x_sum, y_in, y_sum, z_in,
    local_s, core_s, core_r, x_s, x_r, y_s, y_r, z_s, z_r, yg_s, yg_r, xg_s, xg_r, cg_s, cg_r,
    side_s, side_r, bot_s, bot_r,
):
    place = Place()
    core, x, y, z = place.core, place.x, place.y, place.z
    partner, right, down = place.partner(), place.right(), place.down()
    peers = [partner, right, place.left(), down, place.up()]
    peers += [place.along_x(i) for i in range(1, NX)]
    peers += [place.along_y(i) for i in range(1, NY)]
    peers += [place.along_z(i) for i in range(1, NZ)]
    meet(peers)

    first = [
        send(sums.at[q, pl.ds(32 * (1 - core), 32)], core_in.at[q], core_s.at[q], core_r.at[q], partner)
        for q in COMPONENTS
    ]
    side_out = []

    def send_side(k):
        part = (slice(None), pl.ds(F + k * STEP, STEP) if k < CHUNKS else pl.ds(0, F))
        src = grad.at[part + (pl.ds(F, F),)]
        side_out.append(send(src, side.at[part], side_s.at[k], side_r.at[k], right))

    for k in range(CHUNKS):
        send_side(k)
    fetch = pltpu.make_async_copy(grad.at[:, pl.ds(0, EXT), pl.ds(0, F)], main, local_s)
    fetch.start()

    x_out, y_out, z_out = [], [], []
    for q, copy in zip(COMPONENTS, first):
        copy.wait_recv()
        half[q] = sums[q, pl.ds(32 * core, 32)] + core_in[q]
        out = []
        for i in far_first(NX):
            there = lax.rem(x + i, NX)
            part = half.at[q, pl.ds(NY * there, NY)]
            out.append(send(part, x_in.at[q, i - 1], x_s.at[q, i], x_r.at[q, i], place.along_x(i)))
        x_out.append(out)
    for q, copies in zip(COMPONENTS, x_out):
        for copy in copies:
            copy.wait_recv()
        total = half[q, pl.ds(NY * x, NY)]
        for i in range(NX - 1):
            total = total + x_in[q, i]
        x_sum[q] = total
        out = []
        for i in far_first(NY):
            there = lax.rem(y + i, NY)
            part = x_sum.at[q, there]
            out.append(send(part, y_in.at[q, i - 1], y_s.at[q, i], y_r.at[q, i], place.along_y(i)))
        y_out.append(out)
    send_side(CHUNKS)

    fetch.wait()
    first_col = place.col == 0
    bottom_out = []
    for k in range(CHUNKS):
        side_out[k].wait()
        rows = pl.ds(F + k * STEP, STEP)
        extra = jnp.where(first_col, 0.0, side[:, rows, :])
        bottom[:, pl.ds(k * STEP, STEP), :] = main[:, rows, :] + extra
        part = (slice(None), pl.ds(k * STEP, STEP))
        bottom_out.append(send(bottom.at[part], below.at[part], bot_s.at[k], bot_r.at[k], down))

    for q, copies in zip(COMPONENTS, y_out):
        for copy in copies:
            copy.wait_recv()
        total = x_sum[q, y]
        for i in range(NY - 1):
            total = total + y_in[q, i]
        y_sum[q] = total
        z_in[q, z] = total
        out = []
        for i in far_first(NZ):
            out.append(send(y_sum.at[q], z_in.at[q, z], z_s.at[q, i], z_r.at[q, i], place.along_z(i)))
        z_out.append(out)
    done = {}
    for q, copies in zip(COMPONENTS, z_out):
        for copy in copies:
            copy.wait_recv()
        total = z_in[q, 0]
        for i in range(1, NZ):
            total = total + z_in[q, i]
        done[q] = total
    base = 32 * core
    mine = base + NY * x + y
    bar = done[2] + 1.0
    tiles[mine] = probe_tiles[mine] + jnp.concatenate([done[0] / bar, done[1] / bar], 0)

    last = []

    def spread(tile, i):
        out = []
        for j in far_first(NX):
            out.append(send(tiles.at[tile], tiles.at[tile], xg_s.at[i, j], xg_r.at[i, j], place.along_x(j)))
        last.append(send(tiles.at[tile], tiles.at[tile], cg_s.at[i, 0], cg_r.at[i, 0], partner))
        return out

    yg_out, xg_out = {}, {}
    for i in far_first(NY):
        yg_out[i] = send(tiles.at[mine], tiles.at[mine], yg_s.at[i], yg_r.at[i], place.along_y(i))
    xg_out[0] = spread(mine, 0)
    order = sorted(yg_out, key=lambda i: min(i, NY - i))
    for i in order:
        yg_out[i].wait_recv()
        xg_out[i] = spread(base + NY * x + lax.rem(y + NY - i, NY), i)
    for i in [0] + order:
        for j, copy in zip(far_first(NX), xg_out[i]):
            copy.wait_recv()
            tile = base + NY * lax.rem(x + NX - j, NX) + lax.rem(y + NY - i, NY)
            last.append(send(tiles.at[tile], tiles.at[tile], cg_s.at[i, j], cg_r.at[i, j], partner))

    side_out[CHUNKS].wait()
    grad_sum[...] = main[:, pl.ds(0, F), :] + jnp.where(first_col, 0.0, side[:, pl.ds(0, F), :])
    for copy in bottom_out:
        copy.wait()
    first_row = place.row == 0
    grad_sum[:, pl.ds(0, HALO), :] += jnp.where(first_row, 0.0, below[...])
    for copies in [first, *x_out, *y_out, *z_out, yg_out.values(), *xg_out.values()]:
        for copy in copies:
            copy.wait_send()
    for copy in last:
        copy.wait()


def reduce_step(grad, sums, probe_tiles):
    def vmem(*shape):
        return pltpu.VMEM(shape, F32)

    return pl.pallas_call(
        reduce_kernel,
        name="reduce",
        out_shape=(
            jax.ShapeDtypeStruct((2, F, F), F32),
            jax.ShapeDtypeStruct((64, 16, HALF), F32),
        ),
        in_specs=[ANY_SPEC, VMEM_SPEC, VMEM_SPEC],
        out_specs=(VMEM_SPEC, VMEM_SPEC),
        scratch_shapes=[
            vmem(2, EXT, F),
            vmem(2, EXT, F),
            vmem(2, HALO, F),
            vmem(2, HALO, F),
            vmem(3, 32, 8, HALF),
            vmem(3, 32, 8, HALF),
            vmem(3, NX - 1, NY, 8, HALF),
            vmem(3, NY, 8, HALF),
            vmem(3, NY - 1, 8, HALF),
            vmem(3, 8, HALF),
            vmem(3, NZ, 8, HALF),
            DMA,
            *[DMA((3,))] * 2,
            *[DMA((3, NX))] * 2,
            *[DMA((3, NY))] * 2,
            *[DMA((3, NZ))] * 2,
            *[DMA((NY,))] * 2,
            *[DMA((NY, NX))] * 4,
            *[DMA((CHUNKS + 1,))] * 2,
            *[DMA((CHUNKS,))] * 2,
        ],
        compiler_params=pltpu.CompilerParams(
            collective_id=1, has_side_effects=True, vmem_limit_bytes=16 << 20
        ),
    )(grad, sums, probe_tiles)


def finish_kernel(obj, grad_sum, tiles, new_obj, new_probe):
    new_obj[...] = obj[...] + grad_sum[...]
    for t in range(32):
        for h in range(2):
            for c in range(2):
                new_probe[c, 8 * t : 8 * t + 8, HALF * h : HALF * h + HALF] = tiles[
                    2 * t + h, 8 * c : 8 * c + 8
                ]


def finish(obj, grad_sum, tiles):
    out = jax.ShapeDtypeStruct((2, F, F), F32)
    return pl.pallas_call(
        finish_kernel,
        name="finish",
        out_shape=(out, out),
        in_specs=[VMEM_SPEC] * 3,
        out_specs=(VMEM_SPEC, VMEM_SPEC),
        compiler_params=pltpu.CompilerParams(vmem_limit_bytes=12 << 20),
    )(obj, grad_sum, tiles)


def body(object_field, probe_field, measured, positions):
    shared = halo_exchange(object_field, probe_field, measured)
    grad, sums, probe_tiles = frame_step(positions.T, *shared)
    return finish(object_field, *reduce_step(grad, sums, probe_tiles))


def solution(mesh):
    in_specs = (P(None, "row", "col"), P(), P("row", "col", None), P("row", "col"))
    out_specs = (P(None, "row", "col"), P())
    return jax.shard_map(body, mesh=mesh, in_specs=in_specs, out_specs=out_specs, check_vma=False)
```

time: 110 us -> 96.4 us (0.88)
  the two profiles are of different devices: /device:TPU:9 before, /device:TPU:1 now
where the time goes in v2:
time: 96.4 us; the launch traced here: 96.2 us
  Pallas kernels  95.5 us (99%)
    pallas_call x1, Pallas kernels, reduce_step(): pl.pallas_call(reduce_kernel, name='reduce', out_shape=(jax.ShapeDtypeStr...  54.7 us
    pallas_call x1, Pallas kernels, halo_exchange(): pl.pallas_call(halo_kernel, name='halo', out_shape=(like((2, DEEP, 2 * F)...  29.4 us
    pallas_call x1, Pallas kernels, frame_step(): pl.pallas_call(frame_kernel, name='frames', grid=(ampl.shape[0],), out_sh...  10.4 us

profile of v2, /device:TPU:1, one launch (start us, length us, event | category | flops | bytes accessed | tf_op | source)
XLA Modules:
  0.0 96.2 jit_solution(15897105931103605927)
XLA Ops:
  0.6 0.0 copy-start.1
  0.6 29.4 %halo.1 = (f32[2,424,512]{2,1,0:T(8,128)S(1)}, f32[4,256,256]{2,1,0:T(8,128)S(1)}, f32[2,256,256]{2,1,0:T(8,128)S(1)}, bf16[6,256,256]{2,1,0:T(8,128)(2,1)S(1)}, f32[272,128]{1,0:T(8,128)S(1)}) custom-call(f32[2,256,256]{2,1,0:T(8,128)} %obj.3, f32[2,256,256]{2,1,0:T(8,128)} %probe.1, f32[4,256,256]{2,1,0:T(8,128)} %measured.1, ...), custom_call_target="tpu_custom_call" | custom-call | tf_op jit(solution)/shard_map/halo/pallas_call | solution.py:168
  30.1 0.0 copy-done.1
  30.1 10.4 %frames.1 = (f32[2,424,512]{2,1,0:T(8,128)S(1)}, f32[3,64,8,128]{3,2,1,0:T(8,128)S(1)}, f32[64,16,128]{2,1,0:T(8,128)S(1)}) custom-call(s32[2,4]{1,0:T(2,128)S(1)} %bitcast.1, f32[2,424,512]{2,1,0:T(8,128)S(1)} %get-tuple-element.12.ext, f32[4,256,256]{2,1,0:T(8,128)S(1)} %get-tuple-element.13.ampl, f32[2,256,256]{2,1,0:T(8,128)S(1)} %get-tuple-element.14.probe, ...), custom_call_target="tpu_custom_call" | custom-call | tf_op jit(solution)/shard_map/frames/pallas_call | solution.py:327
  40.4 0.0 copy-start
  40.5 54.7 %reduce.1 = (f32[2,256,256]{2,1,0:T(8,128)S(1)}, f32[64,16,128]{2,1,0:T(8,128)S(1)}) custom-call(f32[2,424,512]{2,1,0:T(8,128)S(1)} %get-tuple-element.17.grad, f32[3,64,8,128]{3,2,1,0:T(8,128)S(1)} %get-tuple-element.18.sums, f32[64,16,128]{2,1,0:T(8,128)S(1)} %get-tuple-element.19.probe_tiles), custom_call_target="tpu_custom_call" | custom-call | tf_op jit(solution)/shard_map/reduce/pallas_call | solution.py:482
  95.2 0.0 copy-done
  95.2 1.1 %finish.1 = (f32[2,256,256]{2,1,0:T(8,128)}, f32[2,256,256]{2,1,0:T(8,128)}) custom-call(f32[2,256,256]{2,1,0:T(8,128)S(1)} %copy-done, f32[2,256,256]{2,1,0:T(8,128)S(1)} %get-tuple-element.20.grad_sum, f32[64,16,128]{2,1,0:T(8,128)S(1)} %get-tuple-element.21.tiles), custom_call_target="tpu_custom_call" | custom-call | tf_op jit(solution)/shard_map/finish/pallas_call | solution.py:531
Async XLA Ops:
  0.6 29.4 %copy-start.1 = (s32[4,2]{0,1:T(2,128)S(1)}, s32[4,2]{0,1:T(2,128)}, u32[]{:S(2)}) copy-start(s32[4,2]{0,1:T(2,128)} %param.9) | copy-start | bytes 100
  40.4 54.7 %copy-start = (f32[2,256,256]{2,1,0:T(8,128)S(1)}, f32[2,256,256]{2,1,0:T(8,128)}, u32[]{:S(2)}) copy-start(f32[2,256,256]{2,1,0:T(8,128)} %obj.3) | copy-start | bytes 1572868

commit v3 on v2

--- a/solution.py
+++ b/solution.py
@@ -21,7 +21,12 @@
 DEEP = EXT + 8
 STEP = HALO // CHUNKS
 NX, NY, NZ = 4, 8, 12
+NEAR = 4
+FAR = NZ // NEAR
 COMPONENTS = (2, 0, 1)
+BUNDLES = (pl.ds(2, 1), pl.ds(0, 2))
+GROUPS = ((0, (1, 7)), (3, (2, 6)), (5, (3, 5, 4)))
+SLOT_OF = (0, 1, 3, 5, 7, 6, 4, 2)
 F32 = jnp.float32
 BF16 = jnp.bfloat16
 VMEM_SPEC = pl.BlockSpec(memory_space=pltpu.VMEM)
@@ -51,8 +56,12 @@
     def along_y(self, i):
         return self.at(self.x, lax.rem(self.y + i, NY), self.z, self.core)
 
-    def along_z(self, i):
-        return self.at(self.x, self.y, lax.rem(self.z + i, NZ), self.core)
+    def near_z(self, i):
+        z = NEAR * lax.div(self.z, NEAR) + lax.rem(self.z + i, NEAR)
+        return self.at(self.x, self.y, z, self.core)
+
+    def far_z(self, i):
+        return self.at(self.x, self.y, lax.rem(self.z + NEAR * i, NZ), self.core)
 
     def up(self):
         return (lax.rem(self.row + self.rows - 1, self.rows), self.col)
@@ -236,9 +245,9 @@
 def frame_kernel(
     pos, ext, ampl, probe, mats, twiddle, grad, sums, probe_tiles, acc, scale
 ):
-    frame = pl.program_id(0)
-
-    @pl.when(frame == 0)
+    step = pl.program_id(0)
+
+    @pl.when(step == 0)
     def _():
         grad[...] = jnp.zeros_like(grad)
         acc[...] = jnp.zeros_like(acc)
@@ -253,64 +262,65 @@
                         c, 8 * t : 8 * t + 8, HALF * h : HALF * h + HALF
                     ]
 
-    dy, dx = pos[0, frame], pos[1, frame]
-    r_dy, r_dx = lax.rem(dy, 8), lax.rem(dx, HALF)
-    rows = pl.ds(pl.multiple_of(dy - r_dy, 8), TALL)
-    lanes = pl.ds(pl.multiple_of(dx - r_dx, HALF), WIDE)
-    back_dy, back_dx = lax.rem(TALL - r_dy, TALL), lax.rem(WIDE - r_dx, WIDE)
-
-    def window(c):
-        return pltpu.roll(pltpu.roll(ext[c, rows, lanes], back_dx, 1)[:, :F], back_dy, 0)[:F]
-
-    o_re, o_im = window(0), window(1)
-    p_re, p_im = probe[0], probe[1]
-    t1_high, t1_low, t2_high, t2_low = (mats[i] for i in range(4))
-    down_c = jnp.concatenate([twiddle[:HALF]] * 2, 1)
-    down_s = jnp.concatenate([twiddle[HALF:F]] * 2, 1)
-    over_c, over_s = twiddle[F : F + 1], twiddle[F + 8 : F + 9]
-
-    w_re = p_re * o_re - p_im * o_im
-    w_im = p_re * o_im + p_im * o_re
-    d_re, d_im = w_re[:HALF] - w_re[HALF:], w_im[:HALF] - w_im[HALF:]
-    a = jnp.concatenate([w_re[:HALF] + w_re[HALF:], w_im[:HALF] + w_im[HALF:]], 0)
-    b = jnp.concatenate([d_re * down_c + d_im * down_s, d_im * down_c - d_re * down_s], 0)
-    y_even, y_odd = left_mult(t1_high, t1_low, a), left_mult(t1_high, t1_low, b)
-    x_re = jnp.concatenate([y_even[:HALF], y_odd[:HALF]], 0)
-    x_im = jnp.concatenate([y_even[HALF:], y_odd[HALF:]], 0)
-    d_re, d_im = x_re[:, :HALF] - x_re[:, HALF:], x_im[:, :HALF] - x_im[:, HALF:]
-    a = jnp.concatenate([x_re[:, :HALF] + x_re[:, HALF:], x_im[:, :HALF] + x_im[:, HALF:]], 1)
-    b = jnp.concatenate([d_re * over_c + d_im * over_s, d_im * over_c - d_re * over_s], 1)
-
-    def fit(x, target):
-        re, im = x[:, :HALF], x[:, HALF:]
-        factor = target * jnp.minimum(lax.rsqrt(re * re + im * im), 2.0) - 1.0
-        return jnp.concatenate([re * factor, im * factor], 1)
-
-    s_even = fit(right_mult(a, t2_high, t2_low), ampl[0, :, :HALF])
-    s_odd = fit(right_mult(b, t2_high, t2_low), ampl[0, :, HALF:])
-    e, o = right_mult(s_even, t1_high, t1_low), right_mult(s_odd, t1_high, t1_low)
-    e_re, e_im, o_re2, o_im2 = e[:, :HALF], e[:, HALF:], o[:, :HALF], o[:, HALF:]
-    q_re, q_im = o_re2 * over_c - o_im2 * over_s, o_im2 * over_c + o_re2 * over_s
-    x_re = jnp.concatenate([e_re + q_re, e_re - q_re], 1)
-    x_im = jnp.concatenate([e_im + q_im, e_im - q_im], 1)
-    e = left_mult(t2_high, t2_low, jnp.concatenate([x_re[:HALF], x_im[:HALF]], 0))
-    o = left_mult(t2_high, t2_low, jnp.concatenate([x_re[HALF:], x_im[HALF:]], 0))
-    e_re, e_im, o_re2, o_im2 = e[:HALF], e[HALF:], o[:HALF], o[HALF:]
-    q_re, q_im = o_re2 * down_c - o_im2 * down_s, o_im2 * down_c + o_re2 * down_s
-    c_re = jnp.concatenate([e_re + q_re, e_re - q_re], 0)
-    c_im = jnp.concatenate([e_im + q_im, e_im - q_im], 0)
-
-    acc[0] += o_re * c_re + o_im * c_im
-    acc[1] += o_re * c_im - o_im * c_re
-    acc[2] += o_re * o_re + o_im * o_im
-    inverse = scale[0:1, 0:1]
-    blank_rows, blank_lanes = jnp.zeros((TALL - F, F), F32), jnp.zeros((TALL, WIDE - F), F32)
-    for c, g in ((0, p_re * c_re + p_im * c_im), (1, p_re * c_im - p_im * c_re)):
-        moved = pltpu.roll(jnp.concatenate([g * inverse, blank_rows], 0), r_dy, 0)
-        moved = pltpu.roll(jnp.concatenate([moved, blank_lanes], 1), r_dx, 1)
-        grad[c, rows, lanes] += moved
-
-    @pl.when(frame == pl.num_programs(0) - 1)
+    for k in range(2):
+        dy, dx = pos[0, 2 * step + k], pos[1, 2 * step + k]
+        r_dy, r_dx = lax.rem(dy, 8), lax.rem(dx, HALF)
+        rows = pl.ds(pl.multiple_of(dy - r_dy, 8), TALL)
+        lanes = pl.ds(pl.multiple_of(dx - r_dx, HALF), WIDE)
+        back_dy, back_dx = lax.rem(TALL - r_dy, TALL), lax.rem(WIDE - r_dx, WIDE)
+
+        def window(c):
+            return pltpu.roll(pltpu.roll(ext[c, rows, lanes], back_dx, 1)[:, :F], back_dy, 0)[:F]
+
+        o_re, o_im = window(0), window(1)
+        p_re, p_im = probe[0], probe[1]
+        t1_high, t1_low, t2_high, t2_low = (mats[i] for i in range(4))
+        down_c = jnp.concatenate([twiddle[:HALF]] * 2, 1)
+        down_s = jnp.concatenate([twiddle[HALF:F]] * 2, 1)
+        over_c, over_s = twiddle[F : F + 1], twiddle[F + 8 : F + 9]
+
+        w_re = p_re * o_re - p_im * o_im
+        w_im = p_re * o_im + p_im * o_re
+        d_re, d_im = w_re[:HALF] - w_re[HALF:], w_im[:HALF] - w_im[HALF:]
+        a = jnp.concatenate([w_re[:HALF] + w_re[HALF:], w_im[:HALF] + w_im[HALF:]], 0)
+        b = jnp.concatenate([d_re * down_c + d_im * down_s, d_im * down_c - d_re * down_s], 0)
+        y_even, y_odd = left_mult(t1_high, t1_low, a), left_mult(t1_high, t1_low, b)
+        x_re = jnp.concatenate([y_even[:HALF], y_odd[:HALF]], 0)
+        x_im = jnp.concatenate([y_even[HALF:], y_odd[HALF:]], 0)
+        d_re, d_im = x_re[:, :HALF] - x_re[:, HALF:], x_im[:, :HALF] - x_im[:, HALF:]
+        a = jnp.concatenate([x_re[:, :HALF] + x_re[:, HALF:], x_im[:, :HALF] + x_im[:, HALF:]], 1)
+        b = jnp.concatenate([d_re * over_c + d_im * over_s, d_im * over_c - d_re * over_s], 1)
+
+        def fit(x, target):
+            re, im = x[:, :HALF], x[:, HALF:]
+            factor = target * jnp.minimum(lax.rsqrt(re * re + im * im), 2.0) - 1.0
+            return jnp.concatenate([re * factor, im * factor], 1)
+
+        s_even = fit(right_mult(a, t2_high, t2_low), ampl[k, :, :HALF])
+        s_odd = fit(right_mult(b, t2_high, t2_low), ampl[k, :, HALF:])
+        e, o = right_mult(s_even, t1_high, t1_low), right_mult(s_odd, t1_high, t1_low)
+        e_re, e_im, o_re2, o_im2 = e[:, :HALF], e[:, HALF:], o[:, :HALF], o[:, HALF:]
+        q_re, q_im = o_re2 * over_c - o_im2 * over_s, o_im2 * over_c + o_re2 * over_s
+        x_re = jnp.concatenate([e_re + q_re, e_re - q_re], 1)
+        x_im = jnp.concatenate([e_im + q_im, e_im - q_im], 1)
+        e = left_mult(t2_high, t2_low, jnp.concatenate([x_re[:HALF], x_im[:HALF]], 0))
+        o = left_mult(t2_high, t2_low, jnp.concatenate([x_re[HALF:], x_im[HALF:]], 0))
+        e_re, e_im, o_re2, o_im2 = e[:HALF], e[HALF:], o[:HALF], o[HALF:]
+        q_re, q_im = o_re2 * down_c - o_im2 * down_s, o_im2 * down_c + o_re2 * down_s
+        c_re = jnp.concatenate([e_re + q_re, e_re - q_re], 0)
+        c_im = jnp.concatenate([e_im + q_im, e_im - q_im], 0)
+
+        acc[0] += o_re * c_re + o_im * c_im
+        acc[1] += o_re * c_im - o_im * c_re
+        acc[2] += o_re * o_re + o_im * o_im
+        inverse = scale[0:1, 0:1]
+        blank_rows, blank_lanes = jnp.zeros((TALL - F, F), F32), jnp.zeros((TALL, WIDE - F), F32)
+        for c, g in ((0, p_re * c_re + p_im * c_im), (1, p_re * c_im - p_im * c_re)):
+            moved = pltpu.roll(jnp.concatenate([g * inverse, blank_rows], 0), r_dy, 0)
+            moved = pltpu.roll(jnp.concatenate([moved, blank_lanes], 1), r_dx, 1)
+            grad[c, rows, lanes] += moved
+
+    @pl.when(step == pl.num_programs(0) - 1)
     def _():
         for t in range(32):
             for h in range(2):
@@ -327,7 +337,7 @@
     return pl.pallas_call(
         frame_kernel,
         name="frames",
-        grid=(ampl.shape[0],),
+        grid=(ampl.shape[0] // 2,),
         out_shape=(
             jax.ShapeDtypeStruct((2, DEEP, 2 * F), F32),
             jax.ShapeDtypeStruct((3, 64, 8, HALF), F32),
@@ -336,7 +346,7 @@
         in_specs=[
             pl.BlockSpec(memory_space=pltpu.SMEM),
             whole((2, DEEP, 2 * F)),
-            pl.BlockSpec((1, F, F), lambda f: (f, 0, 0)),
+            pl.BlockSpec((2, F, F), lambda f: (f, 0, 0)),
             whole((2, F, F)),
             whole(mats.shape),
             whole(twiddle.shape),
@@ -349,8 +359,8 @@
 
 def reduce_kernel(
     grad, sums, probe_tiles, grad_sum, tiles,
-    main, side, below, bottom, core_in, half, x_in, x_sum, y_in, y_sum, z_in,
-    local_s, core_s, core_r, x_s, x_r, y_s, y_r, z_s, z_r, yg_s, yg_r, xg_s, xg_r, cg_s, cg_r,
+    main, side, below, bottom, core_in, half, x_in, x_sum, y_in, y_sum, near_in, near_sum, far_in,
+    local_s, core_s, core_r, x_s, x_r, y_s, y_r, n_s, n_r, f_s, f_r, yg_s, yg_r, xg_s, xg_r, cg_s, cg_r,
     side_s, side_r, bot_s, bot_r,
 ):
     place = Place()
@@ -359,7 +369,8 @@
     peers = [partner, right, place.left(), down, place.up()]
     peers += [place.along_x(i) for i in range(1, NX)]
     peers += [place.along_y(i) for i in range(1, NY)]
-    peers += [place.along_z(i) for i in range(1, NZ)]
+    peers += [place.near_z(i) for i in range(1, NEAR)]
+    peers += [place.far_z(i) for i in range(1, FAR)]
     meet(peers)
 
     first = [
@@ -378,7 +389,7 @@
     fetch = pltpu.make_async_copy(grad.at[:, pl.ds(0, EXT), pl.ds(0, F)], main, local_s)
     fetch.start()
 
-    x_out, y_out, z_out = [], [], []
+    x_out, y_out, near_out, far_out = [], [], [], []
     for q, copy in zip(COMPONENTS, first):
         copy.wait_recv()
         half[q] = sums[q, pl.ds(32 * core, 32)] + core_in[q]
@@ -388,18 +399,20 @@
             part = half.at[q, pl.ds(NY * there, NY)]
             out.append(send(part, x_in.at[q, i - 1], x_s.at[q, i], x_r.at[q, i], place.along_x(i)))
         x_out.append(out)
-    for q, copies in zip(COMPONENTS, x_out):
-        for copy in copies:
-            copy.wait_recv()
-        total = half[q, pl.ds(NY * x, NY)]
-        for i in range(NX - 1):
-            total = total + x_in[q, i]
-        x_sum[q] = total
+    waiting = dict(zip(COMPONENTS, x_out))
+    for b, bundle in enumerate(BUNDLES):
+        for q in ((2,), (0, 1))[b]:
+            for copy in waiting[q]:
+                copy.wait_recv()
+            total = half[q, pl.ds(NY * x, NY)]
+            for i in range(NX - 1):
+                total = total + x_in[q, i]
+            x_sum[q] = total
         out = []
         for i in far_first(NY):
             there = lax.rem(y + i, NY)
-            part = x_sum.at[q, there]
-            out.append(send(part, y_in.at[q, i - 1], y_s.at[q, i], y_r.at[q, i], place.along_y(i)))
+            part, dst = x_sum.at[bundle, there], y_in.at[bundle, i - 1]
+            out.append(send(part, dst, y_s.at[b, i], y_r.at[b, i], place.along_y(i)))
         y_out.append(out)
     send_side(CHUNKS)
 
@@ -414,53 +427,66 @@
         part = (slice(None), pl.ds(k * STEP, STEP))
         bottom_out.append(send(bottom.at[part], below.at[part], bot_s.at[k], bot_r.at[k], down))
 
-    for q, copies in zip(COMPONENTS, y_out):
+    in_near, in_far = lax.rem(z, NEAR), lax.div(z, NEAR)
+    for b, bundle in enumerate(BUNDLES):
+        for copy in y_out[b]:
+            copy.wait_recv()
+        total = x_sum[bundle, y]
+        for i in range(NY - 1):
+            total = total + y_in[bundle, i]
+        y_sum[bundle] = total
+        near_in[bundle, in_near] = total
+        out = []
+        for i in range(1, NEAR):
+            dst = near_in.at[bundle, in_near]
+            out.append(send(y_sum.at[bundle], dst, n_s.at[b, i], n_r.at[b, i], place.near_z(i)))
+        near_out.append(out)
+    for b, bundle in enumerate(BUNDLES):
+        for copy in near_out[b]:
+            copy.wait_recv()
+        total = near_in[bundle, 0]
+        for i in range(1, NEAR):
+            total = total + near_in[bundle, i]
+        near_sum[bundle] = total
+        far_in[bundle, in_far] = total
+        out = []
+        for i in range(1, FAR):
+            dst = far_in.at[bundle, in_far]
+            out.append(send(near_sum.at[bundle], dst, f_s.at[b, i], f_r.at[b, i], place.far_z(i)))
+        far_out.append(out)
+    for copies in far_out:
         for copy in copies:
             copy.wait_recv()
-        total = x_sum[q, y]
-        for i in range(NY - 1):
-            total = total + y_in[q, i]
-        y_sum[q] = total
-        z_in[q, z] = total
-        out = []
-        for i in far_first(NZ):
-            out.append(send(y_sum.at[q], z_in.at[q, z], z_s.at[q, i], z_r.at[q, i], place.along_z(i)))
-        z_out.append(out)
-    done = {}
-    for q, copies in zip(COMPONENTS, z_out):
-        for copy in copies:
-            copy.wait_recv()
-        total = z_in[q, 0]
-        for i in range(1, NZ):
-            total = total + z_in[q, i]
-        done[q] = total
+    done = far_in[:, 0]
+    for i in range(1, FAR):
+        done = done + far_in[:, i]
     base = 32 * core
     mine = base + NY * x + y
+    home = base + NY * x
     bar = done[2] + 1.0
-    tiles[mine] = probe_tiles[mine] + jnp.concatenate([done[0] / bar, done[1] / bar], 0)
-
-    last = []
-
-    def spread(tile, i):
+    tiles[home] = probe_tiles[mine] + jnp.concatenate([done[0] / bar, done[1] / bar], 0)
+
+    yg_out = {}
+    for i in far_first(NY):
+        dst = tiles.at[home + SLOT_OF[NY - i]]
+        yg_out[i] = send(tiles.at[home], dst, yg_s.at[i], yg_r.at[i], place.along_y(i))
+    last, xg_out = [], []
+    ends = [start for start, _ in GROUPS[1:]] + [NY]
+    for g, (start, offsets) in enumerate(GROUPS):
+        for offset in offsets:
+            yg_out[NY - offset].wait_recv()
+        part = tiles.at[pl.ds(home + start, ends[g] - start)]
         out = []
         for j in far_first(NX):
-            out.append(send(tiles.at[tile], tiles.at[tile], xg_s.at[i, j], xg_r.at[i, j], place.along_x(j)))
-        last.append(send(tiles.at[tile], tiles.at[tile], cg_s.at[i, 0], cg_r.at[i, 0], partner))
-        return out
-
-    yg_out, xg_out = {}, {}
-    for i in far_first(NY):
-        yg_out[i] = send(tiles.at[mine], tiles.at[mine], yg_s.at[i], yg_r.at[i], place.along_y(i))
-    xg_out[0] = spread(mine, 0)
-    order = sorted(yg_out, key=lambda i: min(i, NY - i))
-    for i in order:
-        yg_out[i].wait_recv()
-        xg_out[i] = spread(base + NY * x + lax.rem(y + NY - i, NY), i)
-    for i in [0] + order:
-        for j, copy in zip(far_first(NX), xg_out[i]):
+            out.append(send(part, part, xg_s.at[g, j], xg_r.at[g, j], place.along_x(j)))
+        xg_out.append(out)
+        last.append(send(part, part, cg_s.at[g, 0], cg_r.at[g, 0], partner))
+    for g, (start, _) in enumerate(GROUPS):
+        for j, copy in zip(far_first(NX), xg_out[g]):
             copy.wait_recv()
-            tile = base + NY * lax.rem(x + NX - j, NX) + lax.rem(y + NY - i, NY)
-            last.append(send(tiles.at[tile], tiles.at[tile], cg_s.at[i, j], cg_r.at[i, j], partner))
+            there = base + NY * lax.rem(x + NX - j, NX) + start
+            part = tiles.at[pl.ds(there, ends[g] - start)]
+            last.append(send(part, part, cg_s.at[g, j], cg_r.at[g, j], partner))
 
     side_out[CHUNKS].wait()
     grad_sum[...] = main[:, pl.ds(0, F), :] + jnp.where(first_col, 0.0, side[:, pl.ds(0, F), :])
@@ -468,7 +494,7 @@
         copy.wait()
     first_row = place.row == 0
     grad_sum[:, pl.ds(0, HALO), :] += jnp.where(first_row, 0.0, below[...])
-    for copies in [first, *x_out, *y_out, *z_out, yg_out.values(), *xg_out.values()]:
+    for copies in [first, *x_out, *y_out, *near_out, *far_out, yg_out.values(), *xg_out]:
         for copy in copies:
             copy.wait_send()
     for copy in last:
@@ -499,14 +525,17 @@
             vmem(3, NY, 8, HALF),
             vmem(3, NY - 1, 8, HALF),
             vmem(3, 8, HALF),
-            vmem(3, NZ, 8, HALF),
+            vmem(3, NEAR, 8, HALF),
+            vmem(3, 8, HALF),
+            vmem(3, FAR, 8, HALF),
             DMA,
             *[DMA((3,))] * 2,
             *[DMA((3, NX))] * 2,
-            *[DMA((3, NY))] * 2,
-            *[DMA((3, NZ))] * 2,
+            *[DMA((2, NY))] * 2,
+            *[DMA((2, NEAR))] * 2,
+            *[DMA((2, FAR))] * 2,
             *[DMA((NY,))] * 2,
-            *[DMA((NY, NX))] * 4,
+            *[DMA((len(GROUPS), NX))] * 4,
             *[DMA((CHUNKS + 1,))] * 2,
             *[DMA((CHUNKS,))] * 2,
         ],
@@ -518,12 +547,16 @@
 
 def finish_kernel(obj, grad_sum, tiles, new_obj, new_probe):
     new_obj[...] = obj[...] + grad_sum[...]
-    for t in range(32):
-        for h in range(2):
+    y = Place().y
+    for there in range(NY):
+        off = lax.rem(there + NY - y, NY)
+        late = jnp.where(off > 4, 2 * (NY - off), 2 * off - 1)
+        slot = jnp.where(off == 0, 0, late)
+        for block in range(8):
+            t, h = divmod(NY * block + there, 2)
+            tile = tiles[NY * block + slot]
             for c in range(2):
-                new_probe[c, 8 * t : 8 * t + 8, HALF * h : HALF * h + HALF] = tiles[
-                    2 * t + h, 8 * c : 8 * c + 8
-                ]
+                new_probe[c, 8 * t : 8 * t + 8, HALF * h : HALF * h + HALF] = tile[8 * c : 8 * c + 8]
 
 
 def finish(obj, grad_sum, tiles):

time: 96.4 us -> 89.1 us (0.924)
  the two profiles are of different devices: /device:TPU:1 before, /device:TPU:73 now
where the time goes in v3:
time: 89.1 us; the launch traced here: 88.9 us
  Pallas kernels  88.3 us (99%)
    pallas_call x1, Pallas kernels, reduce_step(): pl.pallas_call(reduce_kernel, name='reduce', out_shape=(jax.ShapeDtypeStr...  60.4 us
    pallas_call x1, Pallas kernels, halo_exchange(): pl.pallas_call(halo_kernel, name='halo', out_shape=(like((2, DEEP, 2 * F)...  17.8 us
    pallas_call x1, Pallas kernels, frame_step(): pl.pallas_call(frame_kernel, name='frames', grid=(ampl.shape[0] // 2,), o...  9.03 us

profile of v3, /device:TPU:73, one launch (start us, length us, event | category | flops | bytes accessed | tf_op | source)
XLA Modules:
  0.0 88.9 jit_solution(13806198399283992990)
XLA Ops:
  0.6 0.0 copy-start.1
  0.6 17.8 %halo.1 = (f32[2,424,512]{2,1,0:T(8,128)S(1)}, f32[4,256,256]{2,1,0:T(8,128)S(1)}, f32[2,256,256]{2,1,0:T(8,128)S(1)}, bf16[6,256,256]{2,1,0:T(8,128)(2,1)S(1)}, f32[272,128]{1,0:T(8,128)S(1)}) custom-call(f32[2,256,256]{2,1,0:T(8,128)} %obj.3, f32[2,256,256]{2,1,0:T(8,128)} %probe.1, f32[4,256,256]{2,1,0:T(8,128)} %measured.1, ...), custom_call_target="tpu_custom_call" | custom-call | tf_op jit(solution)/shard_map/halo/pallas_call | solution.py:177
  18.4 0.0 copy-done.1
  18.4 9.0 %frames.1 = (f32[2,424,512]{2,1,0:T(8,128)S(1)}, f32[3,64,8,128]{3,2,1,0:T(8,128)S(1)}, f32[64,16,128]{2,1,0:T(8,128)S(1)}) custom-call(s32[2,4]{1,0:T(2,128)S(1)} %bitcast.1, f32[2,424,512]{2,1,0:T(8,128)S(1)} %get-tuple-element.12.ext, f32[4,256,256]{2,1,0:T(8,128)S(1)} %get-tuple-element.13.ampl, f32[2,256,256]{2,1,0:T(8,128)S(1)} %get-tuple-element.14.probe, ...), custom_call_target="tpu_custom_call" | custom-call | tf_op jit(solution)/shard_map/frames/pallas_call | solution.py:337
  27.5 0.0 copy-start
  27.5 60.4 %reduce.1 = (f32[2,256,256]{2,1,0:T(8,128)S(1)}, f32[64,16,128]{2,1,0:T(8,128)S(1)}) custom-call(f32[2,424,512]{2,1,0:T(8,128)S(1)} %get-tuple-element.17.grad, f32[3,64,8,128]{3,2,1,0:T(8,128)S(1)} %get-tuple-element.18.sums, f32[64,16,128]{2,1,0:T(8,128)S(1)} %get-tuple-element.19.probe_tiles), custom_call_target="tpu_custom_call" | custom-call | tf_op jit(solution)/shard_map/reduce/pallas_call | solution.py:508
  87.9 0.0 copy-done
  87.9 1.1 %finish.1 = (f32[2,256,256]{2,1,0:T(8,128)}, f32[2,256,256]{2,1,0:T(8,128)}) custom-call(f32[2,256,256]{2,1,0:T(8,128)S(1)} %copy-done, f32[2,256,256]{2,1,0:T(8,128)S(1)} %get-tuple-element.20.grad_sum, f32[64,16,128]{2,1,0:T(8,128)S(1)} %get-tuple-element.21.tiles), custom_call_target="tpu_custom_call" | custom-call | tf_op jit(solution)/shard_map/finish/pallas_call | solution.py:564
Async XLA Ops:
  0.6 17.8 %copy-start.1 = (s32[4,2]{0,1:T(2,128)S(1)}, s32[4,2]{0,1:T(2,128)}, u32[]{:S(2)}) copy-start(s32[4,2]{0,1:T(2,128)} %param.9) | copy-start | bytes 100
  27.5 60.4 %copy-start = (f32[2,256,256]{2,1,0:T(8,128)S(1)}, f32[2,256,256]{2,1,0:T(8,128)}, u32[]{:S(2)}) copy-start(f32[2,256,256]{2,1,0:T(8,128)} %obj.3) | copy-start | bytes 1572868

commit v4 on v3

--- a/solution.py
+++ b/solution.py
@@ -20,6 +20,8 @@
 WIDE = F + 128
 DEEP = EXT + 8
 STEP = HALO // CHUNKS
+PARTS = 10
+PART = HALO // PARTS
 NX, NY, NZ = 4, 8, 12
 NEAR = 4
 FAR = NZ // NEAR
@@ -123,12 +125,16 @@
             )
         )
     ]
+    barrier = pltpu.get_barrier_semaphore()
+    peers = (up, place.down(), left, place.right())
+    for device in peers:
+        pl.semaphore_signal(barrier, inc=1, device_id=device, device_id_type=MESH)
     for load in loads:
         load.start()
-    meet((up, place.down(), left, place.right()))
+    pl.semaphore_wait(barrier, len(peers))
     rows = []
-    for k in range(CHUNKS):
-        here, there = pl.ds(k * STEP, STEP), pl.ds(F + k * STEP, STEP)
+    for k in range(PARTS):
+        here, there = pl.ds(k * PART, PART), pl.ds(F + k * PART, PART)
         dst = ext.at[:, there, pl.ds(0, F)]
         rows.append(send(obj.at[:, here], dst, row_s.at[k], row_r.at[k], up))
     side = send(obj, ext.at[:, pl.ds(0, F), pl.ds(F, F)], col_s, col_r, left)
@@ -145,15 +151,15 @@
     lax.fori_loop(0, raw.shape[0], reorder, 0)
 
     corners = []
-    for k in range(CHUNKS):
-        there = pl.ds(F + k * STEP, STEP)
+    for k in range(PARTS):
+        there = pl.ds(F + k * PART, PART)
         src, dst = ext.at[:, there, pl.ds(0, F)], ext.at[:, there, pl.ds(F, F)]
         rows[k].wait_recv()
         corners.append(send(src, dst, cor_s.at[k], cor_r.at[k], left))
     for load in loads[2:]:
         load.wait()
     side.wait()
-    for k in range(CHUNKS):
+    for k in range(PARTS):
         rows[k].wait_send()
         corners[k].wait()
 
@@ -188,12 +194,12 @@
         out_specs=(VMEM_SPEC,) * 5,
         scratch_shapes=[
             pltpu.VMEM((frames, F, F), F32),
-            DMA((CHUNKS,)),
-            DMA((CHUNKS,)),
+            DMA((PARTS,)),
+            DMA((PARTS,)),
             DMA,
             DMA,
-            DMA((CHUNKS,)),
-            DMA((CHUNKS,)),
+            DMA((PARTS,)),
+            DMA((PARTS,)),
             DMA((5,)),
         ],
         compiler_params=pltpu.CompilerParams(
@@ -267,10 +273,17 @@
         r_dy, r_dx = lax.rem(dy, 8), lax.rem(dx, HALF)
         rows = pl.ds(pl.multiple_of(dy - r_dy, 8), TALL)
         lanes = pl.ds(pl.multiple_of(dx - r_dx, HALF), WIDE)
-        back_dy, back_dx = lax.rem(TALL - r_dy, TALL), lax.rem(WIDE - r_dx, WIDE)
+        lane = lax.broadcasted_iota(jnp.int32, (TALL, HALF), 1)
+        line = lax.broadcasted_iota(jnp.int32, (32, 8, F), 1)
+        back_dy, back_dx = lax.rem(8 - r_dy, 8), lax.rem(HALF - r_dx, HALF)
 
         def window(c):
-            return pltpu.roll(pltpu.roll(ext[c, rows, lanes], back_dx, 1)[:, :F], back_dy, 0)[:F]
+            wide = ext[c, rows, lanes]
+            turned = [pltpu.roll(wide[:, HALF * j : HALF * j + HALF], back_dx, 1) for j in range(3)]
+            keep = lane < HALF - r_dx
+            tall = jnp.concatenate([jnp.where(keep, turned[j], turned[j + 1]) for j in range(2)], 1)
+            tall = pltpu.roll(tall.reshape(33, 8, F), back_dy, 1)
+            return jnp.where(line < 8 - r_dy, tall[:32], tall[1:]).reshape(F, F)
 
         o_re, o_im = window(0), window(1)
         p_re, p_im = probe[0], probe[1]
@@ -314,11 +327,25 @@
         acc[1] += o_re * c_im - o_im * c_re
         acc[2] += o_re * o_re + o_im * o_im
         inverse = scale[0:1, 0:1]
-        blank_rows, blank_lanes = jnp.zeros((TALL - F, F), F32), jnp.zeros((TALL, WIDE - F), F32)
+        blank = jnp.zeros((1, 8, F), F32)
+        edge = jnp.zeros((TALL, HALF), F32)
+        below = lax.broadcasted_iota(jnp.int32, (33, 8, F), 1) >= r_dy
+        beyond = lane >= r_dx
         for c, g in ((0, p_re * c_re + p_im * c_im), (1, p_re * c_im - p_im * c_re)):
-            moved = pltpu.roll(jnp.concatenate([g * inverse, blank_rows], 0), r_dy, 0)
-            moved = pltpu.roll(jnp.concatenate([moved, blank_lanes], 1), r_dx, 1)
-            grad[c, rows, lanes] += moved
+            turned = pltpu.roll((g * inverse).reshape(32, 8, F), r_dy, 1)
+            moved = jnp.where(
+                below, jnp.concatenate([turned, blank], 0), jnp.concatenate([blank, turned], 0)
+            ).reshape(TALL, F)
+            first = pltpu.roll(moved[:, :HALF], r_dx, 1)
+            second = pltpu.roll(moved[:, HALF:], r_dx, 1)
+            grad[c, rows, lanes] += jnp.concatenate(
+                [
+                    jnp.where(beyond, first, edge),
+                    jnp.where(beyond, second, first),
+                    jnp.where(beyond, edge, second),
+                ],
+                1,
+            )
 
     @pl.when(step == pl.num_programs(0) - 1)
     def _():
@@ -366,11 +393,12 @@
     place = Place()
     core, x, y, z = place.core, place.x, place.y, place.z
     partner, right, down = place.partner(), place.right(), place.down()
-    peers = [partner, right, place.left(), down, place.up()]
-    peers += [place.along_x(i) for i in range(1, NX)]
-    peers += [place.along_y(i) for i in range(1, NY)]
-    peers += [place.near_z(i) for i in range(1, NEAR)]
-    peers += [place.far_z(i) for i in range(1, FAR)]
+    peers = [place.far_z(i) for i in range(1, FAR)]
+    peers += [place.along_y(i) for i in far_first(NY)]
+    peers += [place.near_z(i) for i in range(NEAR - 1, 0, -1)]
+    peers += [down, place.up()]
+    peers += [place.along_x(i) for i in far_first(NX)]
+    peers += [place.left(), right, partner]
     meet(peers)
 
     first = [

time: 89.1 us -> 87.7 us (0.984)
  Pallas kernels: 88.3 us -> 86.9 us
    pallas_call x1, Pallas kernels: 9.03 us -> 7.75 us  [frame_step(): pl.pallas_call(frame_kernel, name='frames', grid=(ampl.shape[0] // 2,), o...]
where the time goes in v4:
time: 87.7 us; the launch traced here: 87.6 us
  Pallas kernels  86.9 us (99%)
    pallas_call x1, Pallas kernels, reduce_step(): pl.pallas_call(reduce_kernel, name='reduce', out_shape=(jax.ShapeDtypeStr...  60.4 us
    pallas_call x1, Pallas kernels, halo_exchange(): pl.pallas_call(halo_kernel, name='halo', out_shape=(like((2, DEEP, 2 * F)...  17.6 us
    pallas_call x1, Pallas kernels, frame_step(): pl.pallas_call(frame_kernel, name='frames', grid=(ampl.shape[0] // 2,), o...  7.75 us

profile of v4, /device:TPU:73, one launch (start us, length us, event | category | flops | bytes accessed | tf_op | source)
XLA Modules:
  0.0 87.6 jit_solution(17918764560208270462)
XLA Ops:
  0.6 0.0 copy-start.1
  0.6 17.6 %halo.1 = (f32[2,424,512]{2,1,0:T(8,128)S(1)}, f32[4,256,256]{2,1,0:T(8,128)S(1)}, f32[2,256,256]{2,1,0:T(8,128)S(1)}, bf16[6,256,256]{2,1,0:T(8,128)(2,1)S(1)}, f32[272,128]{1,0:T(8,128)S(1)}) custom-call(f32[2,256,256]{2,1,0:T(8,128)} %obj.3, f32[2,256,256]{2,1,0:T(8,128)} %probe.1, f32[4,256,256]{2,1,0:T(8,128)} %measured.1, ...), custom_call_target="tpu_custom_call" | custom-call | tf_op jit(solution)/shard_map/halo/pallas_call | solution.py:183
  18.2 0.0 copy-done.1
  18.2 7.8 %frames.1 = (f32[2,424,512]{2,1,0:T(8,128)S(1)}, f32[3,64,8,128]{3,2,1,0:T(8,128)S(1)}, f32[64,16,128]{2,1,0:T(8,128)S(1)}) custom-call(s32[2,4]{1,0:T(2,128)S(1)} %bitcast.1, f32[2,424,512]{2,1,0:T(8,128)S(1)} %get-tuple-element.12.ext, f32[4,256,256]{2,1,0:T(8,128)S(1)} %get-tuple-element.13.ampl, f32[2,256,256]{2,1,0:T(8,128)S(1)} %get-tuple-element.14.probe, ...), custom_call_target="tpu_custom_call" | custom-call | tf_op jit(solution)/shard_map/frames/pallas_call | solution.py:364
  26.0 0.0 copy-start
  26.0 60.4 %reduce.1 = (f32[2,256,256]{2,1,0:T(8,128)S(1)}, f32[64,16,128]{2,1,0:T(8,128)S(1)}) custom-call(f32[2,424,512]{2,1,0:T(8,128)S(1)} %get-tuple-element.17.grad, f32[3,64,8,128]{3,2,1,0:T(8,128)S(1)} %get-tuple-element.18.sums, f32[64,16,128]{2,1,0:T(8,128)S(1)} %get-tuple-element.19.probe_tiles), custom_call_target="tpu_custom_call" | custom-call | tf_op jit(solution)/shard_map/reduce/pallas_call | solution.py:536
  86.5 0.0 copy-done
  86.5 1.1 %finish.1 = (f32[2,256,256]{2,1,0:T(8,128)}, f32[2,256,256]{2,1,0:T(8,128)}) custom-call(f32[2,256,256]{2,1,0:T(8,128)S(1)} %copy-done, f32[2,256,256]{2,1,0:T(8,128)S(1)} %get-tuple-element.20.grad_sum, f32[64,16,128]{2,1,0:T(8,128)S(1)} %get-tuple-element.21.tiles), custom_call_target="tpu_custom_call" | custom-call | tf_op jit(solution)/shard_map/finish/pallas_call | solution.py:592
Async XLA Ops:
  0.6 17.6 %copy-start.1 = (s32[4,2]{0,1:T(2,128)S(1)}, s32[4,2]{0,1:T(2,128)}, u32[]{:S(2)}) copy-start(s32[4,2]{0,1:T(2,128)} %param.9) | copy-start | bytes 100
  26.0 60.5 %copy-start = (f32[2,256,256]{2,1,0:T(8,128)S(1)}, f32[2,256,256]{2,1,0:T(8,128)}, u32[]{:S(2)}) copy-start(f32[2,256,256]{2,1,0:T(8,128)} %obj.3) | copy-start | bytes 1572868

commit v5 on v4

--- a/solution.py
+++ b/solution.py
@@ -251,25 +251,20 @@
 def frame_kernel(
     pos, ext, ampl, probe, mats, twiddle, grad, sums, probe_tiles, acc, scale
 ):
-    step = pl.program_id(0)
-
-    @pl.when(step == 0)
-    def _():
-        grad[...] = jnp.zeros_like(grad)
-        acc[...] = jnp.zeros_like(acc)
-        p_re, p_im = probe[0], probe[1]
-        power = jnp.max(p_re * p_re + p_im * p_im, axis=0, keepdims=True)
-        top = jnp.max(power, axis=1, keepdims=True)
-        scale[...] = 1.0 / jnp.broadcast_to(top, scale.shape)
-        for t in range(32):
-            for h in range(2):
-                for c in range(2):
-                    probe_tiles[2 * t + h, 8 * c : 8 * c + 8] = probe[
-                        c, 8 * t : 8 * t + 8, HALF * h : HALF * h + HALF
-                    ]
-
-    for k in range(2):
-        dy, dx = pos[0, 2 * step + k], pos[1, 2 * step + k]
+    grad[...] = jnp.zeros_like(grad)
+    p_re, p_im = probe[0], probe[1]
+    power = jnp.max(p_re * p_re + p_im * p_im, axis=0, keepdims=True)
+    top = jnp.max(power, axis=1, keepdims=True)
+    scale[...] = 1.0 / jnp.broadcast_to(top, scale.shape)
+    for t in range(32):
+        for h in range(2):
+            for c in range(2):
+                probe_tiles[2 * t + h, 8 * c : 8 * c + 8] = probe[
+                    c, 8 * t : 8 * t + 8, HALF * h : HALF * h + HALF
+                ]
+
+    for k in range(ampl.shape[0]):
+        dy, dx = pos[0, k], pos[1, k]
         r_dy, r_dx = lax.rem(dy, 8), lax.rem(dx, HALF)
         rows = pl.ds(pl.multiple_of(dy - r_dy, 8), TALL)
         lanes = pl.ds(pl.multiple_of(dx - r_dx, HALF), WIDE)
@@ -323,9 +318,9 @@
         c_re = jnp.concatenate([e_re + q_re, e_re - q_re], 0)
         c_im = jnp.concatenate([e_im + q_im, e_im - q_im], 0)
 
-        acc[0] += o_re * c_re + o_im * c_im
-        acc[1] += o_re * c_im - o_im * c_re
-        acc[2] += o_re * o_re + o_im * o_im
+        parts = (o_re * c_re + o_im * c_im, o_re * c_im - o_im * c_re, o_re * o_re + o_im * o_im)
+        for c, part in enumerate(parts):
+            acc[c] = part if k == 0 else acc[c] + part
         inverse = scale[0:1, 0:1]
         blank = jnp.zeros((1, 8, F), F32)
         edge = jnp.zeros((TALL, HALF), F32)
@@ -347,24 +342,18 @@
                 1,
             )
 
-    @pl.when(step == pl.num_programs(0) - 1)
-    def _():
-        for t in range(32):
-            for h in range(2):
-                for c in range(3):
-                    sums[c, 2 * t + h] = acc[
-                        c, 8 * t : 8 * t + 8, HALF * h : HALF * h + HALF
-                    ]
+    for t in range(32):
+        for h in range(2):
+            for c in range(3):
+                sums[c, 2 * t + h] = acc[
+                    c, 8 * t : 8 * t + 8, HALF * h : HALF * h + HALF
+                ]
 
 
 def frame_step(positions, ext, ampl, probe, mats, twiddle):
-    def whole(shape):
-        return pl.BlockSpec(shape, lambda f: (0,) * len(shape))
-
     return pl.pallas_call(
         frame_kernel,
         name="frames",
-        grid=(ampl.shape[0] // 2,),
         out_shape=(
             jax.ShapeDtypeStruct((2, DEEP, 2 * F), F32),
             jax.ShapeDtypeStruct((3, 64, 8, HALF), F32),
@@ -372,13 +361,9 @@
         ),
         in_specs=[
             pl.BlockSpec(memory_space=pltpu.SMEM),
-            whole((2, DEEP, 2 * F)),
-            pl.BlockSpec((2, F, F), lambda f: (f, 0, 0)),
-            whole((2, F, F)),
-            whole(mats.shape),
-            whole(twiddle.shape),
+            *[VMEM_SPEC] * 5,
         ],
-        out_specs=(whole((2, DEEP, 2 * F)), whole((3, 64, 8, HALF)), whole((64, 16, HALF))),
+        out_specs=(VMEM_SPEC,) * 3,
         scratch_shapes=[pltpu.VMEM((3, F, F), F32), pltpu.VMEM((8, HALF), F32)],
         compiler_params=pltpu.CompilerParams(vmem_limit_bytes=28 << 20),
     )(positions, ext, ampl, probe, mats, twiddle)

time: 87.7 us -> 86.8 us (0.990)
  Pallas kernels: 86.9 us -> 85.9 us
    pallas_call x1, Pallas kernels: 7.75 us -> 6.86 us  [frame_step(): pl.pallas_call(frame_kernel, name='frames', out_shape=(jax.ShapeDtypeStru...]
where the time goes in v5:
time: 86.8 us; the launch traced here: 86.6 us
  Pallas kernels  85.9 us (99%)
    pallas_call x1, Pallas kernels, reduce_step(): pl.pallas_call(reduce_kernel, name='reduce', out_shape=(jax.ShapeDtypeStr...  60.4 us
    pallas_call x1, Pallas kernels, halo_exchange(): pl.pallas_call(halo_kernel, name='halo', out_shape=(like((2, DEEP, 2 * F)...  17.6 us
    pallas_call x1, Pallas kernels, frame_step(): pl.pallas_call(frame_kernel, name='frames', out_shape=(jax.ShapeDtypeStru...  6.86 us

profile of v5, /device:TPU:73, one launch (start us, length us, event | category | flops | bytes accessed | tf_op | source)
XLA Modules:
  0.0 86.6 jit_solution(61896302055585810)
XLA Ops:
  0.6 0.0 copy-start.1
  0.6 17.6 %halo.1 = (f32[2,424,512]{2,1,0:T(8,128)S(1)}, f32[4,256,256]{2,1,0:T(8,128)S(1)}, f32[2,256,256]{2,1,0:T(8,128)S(1)}, bf16[6,256,256]{2,1,0:T(8,128)(2,1)S(1)}, f32[272,128]{1,0:T(8,128)S(1)}) custom-call(f32[2,256,256]{2,1,0:T(8,128)} %obj.3, f32[2,256,256]{2,1,0:T(8,128)} %probe.1, f32[4,256,256]{2,1,0:T(8,128)} %measured.1, ...), custom_call_target="tpu_custom_call" | custom-call | tf_op jit(solution)/shard_map/halo/pallas_call | solution.py:183
  18.2 0.0 copy-done.1
  18.2 6.9 %frames.1 = (f32[2,424,512]{2,1,0:T(8,128)S(1)}, f32[3,64,8,128]{3,2,1,0:T(8,128)S(1)}, f32[64,16,128]{2,1,0:T(8,128)S(1)}) custom-call(s32[2,4]{1,0:T(2,128)S(1)} %bitcast.1, f32[2,424,512]{2,1,0:T(8,128)S(1)} %get-tuple-element.12.ext, f32[4,256,256]{2,1,0:T(8,128)S(1)} %get-tuple-element.13.ampl, f32[2,256,256]{2,1,0:T(8,128)S(1)} %get-tuple-element.14.probe, ...), custom_call_target="tpu_custom_call" | custom-call | tf_op jit(solution)/shard_map/frames/pallas_call | solution.py:354
  25.1 0.0 copy-start
  25.1 60.4 %reduce.1 = (f32[2,256,256]{2,1,0:T(8,128)S(1)}, f32[64,16,128]{2,1,0:T(8,128)S(1)}) custom-call(f32[2,424,512]{2,1,0:T(8,128)S(1)} %get-tuple-element.17.grad, f32[3,64,8,128]{3,2,1,0:T(8,128)S(1)} %get-tuple-element.18.sums, f32[64,16,128]{2,1,0:T(8,128)S(1)} %get-tuple-element.19.probe_tiles), custom_call_target="tpu_custom_call" | custom-call | tf_op jit(solution)/shard_map/reduce/pallas_call | solution.py:521
  85.5 0.0 copy-done
  85.5 1.1 %finish.1 = (f32[2,256,256]{2,1,0:T(8,128)}, f32[2,256,256]{2,1,0:T(8,128)}) custom-call(f32[2,256,256]{2,1,0:T(8,128)S(1)} %copy-done, f32[2,256,256]{2,1,0:T(8,128)S(1)} %get-tuple-element.20.grad_sum, f32[64,16,128]{2,1,0:T(8,128)S(1)} %get-tuple-element.21.tiles), custom_call_target="tpu_custom_call" | custom-call | tf_op jit(solution)/shard_map/finish/pallas_call | solution.py:577
Async XLA Ops:
  0.6 17.6 %copy-start.1 = (s32[4,2]{0,1:T(2,128)S(1)}, s32[4,2]{0,1:T(2,128)}, u32[]{:S(2)}) copy-start(s32[4,2]{0,1:T(2,128)} %param.9) | copy-start | bytes 100
  25.1 60.4 %copy-start = (f32[2,256,256]{2,1,0:T(8,128)S(1)}, f32[2,256,256]{2,1,0:T(8,128)}, u32[]{:S(2)}) copy-start(f32[2,256,256]{2,1,0:T(8,128)} %obj.3) | copy-start | bytes 1572868
